TPU v7x, 32 devices: a whole 2x2x4 slice. The times are simulated.
32 devices in a mesh: freq: 4 (over y, x), tile: 8 (over z, core).
Axes of the slice: x: 2, y: 2, z: 4, core: 2. Of those that a mesh axis runs over, the one named last changes fastest.
Arguments:
- voltages: bfloat16 [4096, 24960], P(('freq', 'tile')), may hold values from -16 to 16, as said below
- channel_ids: int32 [12], replicated, may hold values from 1 to 63
- start_basis: float32 [2, 8, 4096], replicated, may hold values from -0.0625 to 0.0625
Outputs:
- cleaned: float32 [2, 12, 192, 4096], P(None, 'freq', 'tile')
Inputs may be any that keep to these rules, and one draw needn't show every extreme that they name: `voltages`: real samples of each input over the whole window.
All inputs are finite; a program needn't handle non-finite values.
Results may differ from a plain program's by a relative error of at most 0.0048.
Values may be sent and summed in bfloat16 or wider, within the bound.
A program may use at most 128 MiB of HBM per device.

v0:
```python
import functools
import math

import jax
import jax.numpy as jnp
from jax import lax
from jax.experimental import pallas as pl
from jax.experimental.pallas import tpu as pltpu
from jax.sharding import PartitionSpec as P

TAPS = 4
P_SIZE = 128
ITERS = 3
STEP = 16

loading = 0.5
highest = lax.Precision.HIGHEST
VMEM = pl.BlockSpec(memory_space=pltpu.VMEM)
MESH = pl.DeviceIdType.MESH


def make_table(channel_ids, taps_count, points):
    length = taps_count * points
    offsets = jnp.arange(length, dtype=jnp.float32)
    shifted = (offsets + 0.5 - length / 2.0) / points
    window = jnp.sinc(shifted) * (0.5 - 0.5 * jnp.cos(2.0 * math.pi * (offsets + 0.5) / length))
    window = window / jnp.sqrt(jnp.sum(window * window))
    window = window.reshape(taps_count, points)
    phases = channel_ids[:, None] * jnp.arange(points, dtype=jnp.int32)[None, :] % points
    angles = 2.0 * math.pi / points * phases.astype(jnp.float32)
    rotors = jnp.stack([jnp.cos(angles), -jnp.sin(angles)])
    return (window[:, None, None, :] * rotors[None]).astype(jnp.bfloat16)


def banded(coeffs):
    rows = coeffs.shape[1]
    spect = lax.broadcasted_iota(jnp.int32, (1, STEP, STEP + TAPS - 1, 1), 1)
    frame = lax.broadcasted_iota(jnp.int32, (1, STEP, STEP + TAPS - 1, 1), 2)
    table = jnp.zeros((rows, STEP, STEP + TAPS - 1, P_SIZE), jnp.bfloat16)
    for tap in range(TAPS):
        table = jnp.where(frame - spect == tap, coeffs[tap][:, None, None, :], table)
    return table.reshape(rows * STEP, (STEP + TAPS - 1) * P_SIZE)


def nt(left, right):
    return lax.dot_general(left, right, (((1,), (1,)), ((), ())), preferred_element_type=jnp.float32)


def split3(value):
    high = value.astype(jnp.bfloat16)
    rest = value - high.astype(jnp.float32)
    mid = rest.astype(jnp.bfloat16)
    low = (rest - mid.astype(jnp.float32)).astype(jnp.bfloat16)
    return jnp.concatenate([high, mid, low], axis=0)


def fold3(value):
    rows = value.shape[0] // 3
    return value[:rows] + value[rows : 2 * rows] + value[2 * rows :]


def plain(left, right):
    return lax.dot_general(left, right, (((1,), (0,)), ((), ())), preferred_element_type=jnp.float32)


def project(z, real_v, imag_v, k):
    parts = split3(z)
    on_re = fold3(nt(parts, real_v))
    on_im = fold3(nt(parts, imag_v))
    return jnp.concatenate([on_re[:k] + on_im[k:], on_re[k:] - on_im[:k]], axis=0)


def inverse_factor(gram, k, off=0):
    lanes = gram.shape[1]
    col = lax.broadcasted_iota(jnp.int32, (k, lanes), 1)
    row = lax.broadcasted_iota(jnp.int32, (k, lanes), 0)
    zero = jnp.zeros((k, lanes), jnp.float32)
    a_re = gram[:k]
    a_im = gram[k:]
    m_re = jnp.where(col == row, 1.0, zero)
    m_im = zero
    for j in range(k):
        at_col = col == j + off
        c_re = jnp.sum(jnp.where(at_col, a_re, 0.0), axis=1, keepdims=True)
        c_im = jnp.sum(jnp.where(at_col, a_im, 0.0), axis=1, keepdims=True)
        pivot = jnp.sqrt(c_re[j : j + 1])
        l_re = jnp.where(row[:, :1] > j, c_re / pivot, 0.0)
        l_im = jnp.where(row[:, :1] > j, c_im / pivot, 0.0)
        ar, ai = a_re[j : j + 1] / pivot, a_im[j : j + 1] / pivot
        mr, mi = m_re[j : j + 1] / pivot, m_im[j : j + 1] / pivot
        here = row == j
        a_re = jnp.where(here, ar, a_re - (l_re * ar - l_im * ai))
        a_im = jnp.where(here, ai, a_im - (l_re * ai + l_im * ar))
        m_re = jnp.where(here, mr, m_re - (l_re * mr - l_im * mi))
        m_im = jnp.where(here, mi, m_im - (l_re * mi + l_im * mr))
    return m_re, -m_im


def mix(m_re, m_im, rows, k):
    out_re = jnp.zeros((k, rows.shape[1]), jnp.float32)
    out_im = jnp.zeros((k, rows.shape[1]), jnp.float32)
    for j in range(k):
        f_re, f_im = m_re[:, j : j + 1], m_im[:, j : j + 1]
        r_re, r_im = rows[j : j + 1], rows[k + j : k + j + 1]
        out_re = out_re + (f_re * r_re - f_im * r_im)
        out_im = out_im + (f_re * r_im + f_im * r_re)
    return jnp.concatenate([out_re, out_im], axis=0)


def tn(left, right):
    return lax.dot_general(left, right, (((0,), (0,)), ((), ())), preferred_element_type=jnp.float32)


def fused_kernel(
    volts_ref, table_ref, start_ref, out_ref,
    stage, v_ref, z_ref, part_ref, land_ref, sum_ref, give_ref,
    f_send, f_recv, r_send, r_recv, g_send, g_recv, o_send, o_recv, own_sem,
    *, k, freq, tile, base, off,
):
    chans, _, spectra, width = v_ref.shape
    cols = volts_ref.shape[0]
    steps = spectra // STEP
    block = spectra // tile
    chunk = part_ref.shape[1] // tile
    group = lax.axis_index("freq")
    me = lax.axis_index("tile")
    barrier = pltpu.get_barrier_semaphore()
    for d in range(1, freq):
        pl.semaphore_signal(barrier, inc=1, device_id={"freq": lax.rem(group + d, freq)}, device_id_type=MESH)
    for d in range(1, tile):
        pl.semaphore_signal(barrier, inc=1, device_id={"tile": lax.rem(me + d, tile)}, device_id_type=MESH)
    pl.semaphore_wait(barrier, freq - 1 + tile - 1)

    span = (STEP + TAPS - 1) * P_SIZE
    my_cols = pl.ds(pl.multiple_of(group * cols, cols), cols)

    def handover(i, d):
        peer = lax.rem(group + d, freq)
        rows = pl.ds(pl.multiple_of(i * STEP, STEP), STEP)
        return pltpu.make_async_remote_copy(
            src_ref=stage.at[peer, :, :, rows, :],
            dst_ref=v_ref.at[:, :, rows, my_cols],
            send_sem=f_send.at[i, d - 1],
            recv_sem=f_recv.at[i, d - 1],
            device_id={"freq": peer},
            device_id_type=MESH,
        )

    def own_part(i):
        rows = pl.ds(pl.multiple_of(i * STEP, STEP), STEP)
        return pltpu.make_async_copy(
            stage.at[group, :, :, rows, :], v_ref.at[:, :, rows, my_cols], own_sem.at[i]
        )

    def filter_step(i, carry):
        start = pl.multiple_of(i * (STEP * P_SIZE), P_SIZE)
        result = nt(table_ref[...], volts_ref[:, pl.ds(start, span)])
        rows = pl.ds(pl.multiple_of(i * STEP, STEP), STEP)
        stage[:, :, :, rows, :] = result.reshape(freq, chans, 2, STEP, cols).astype(jnp.bfloat16)
        for d in range(1, freq):
            handover(i, d).start()
        own_part(i).start()
        return carry

    lax.fori_loop(0, steps, filter_step, 0)

    def filter_wait(i, carry):
        for d in range(1, freq):
            handover(i, d).wait()
        own_part(i).wait()
        return carry

    lax.fori_loop(0, steps, filter_wait, 0)

    mine = pl.ds(pl.multiple_of(me * chunk, 8), chunk)

    def tile_sum(at):
        sends = []
        for d in range(1, tile):
            peer = lax.rem(me + d, tile)
            copy = pltpu.make_async_remote_copy(
                src_ref=part_ref.at[at, pl.ds(pl.multiple_of(peer * chunk, 8), chunk)],
                dst_ref=land_ref.at[at, d - 1],
                send_sem=r_send.at[at, d - 1],
                recv_sem=r_recv.at[at, d - 1],
                device_id={"tile": peer},
                device_id_type=MESH,
            )
            copy.start()
            sends.append(copy)
        total = part_ref[at, mine]
        for d in range(1, tile):
            sends[d - 1].wait_recv()
            total = total + land_ref[at, d - 1]
        sum_ref[at, mine] = total
        for d in range(1, tile):
            copy = pltpu.make_async_remote_copy(
                src_ref=sum_ref.at[at, mine],
                dst_ref=sum_ref.at[at, mine],
                send_sem=g_send.at[at, d - 1],
                recv_sem=g_recv.at[at, d - 1],
                device_id={"tile": lax.rem(me + d, tile)},
                device_id_type=MESH,
            )
            copy.start()
            sends.append(copy)
        for copy in sends[tile - 1 :]:
            copy.wait_recv()
        return sends

    def rows_of(c):
        return slice(2 * k * c, 2 * k * (c + 1))

    part_ref[...] = jnp.zeros_like(part_ref)
    for c in range(chans):
        part_ref[0, rows_of(c), :spectra] = project(start_ref[...], v_ref[c, 0], v_ref[c, 1], k)
    pending = tile_sum(0)
    for step_at in range(ITERS):
        for c in range(chans):
            weights = sum_ref[step_at, rows_of(c), :spectra]
            if step_at == 0:
                basis = start_ref[...]
            else:
                m_re, m_im = inverse_factor(sum_ref[step_at, rows_of(c), base:], k, off)
                weights = mix(m_re, m_im, weights, k)
                basis = mix(m_re, m_im, z_ref[c], k)
            real_v, imag_v = v_ref[c, 0], v_ref[c, 1]
            parts = split3(weights / spectra)
            on_re = fold3(plain(parts, real_v))
            on_im = fold3(plain(parts, imag_v))
            z = jnp.concatenate([on_re[:k] - on_im[k:], on_re[k:] + on_im[:k]], axis=0) + loading * basis
            z_ref[c] = z
            before = [jnp.zeros((off, width), jnp.float32)] if off else []
            after = jnp.zeros((128 - off - k, width), jnp.float32)
            dims = (((1,), (1,)), ((), ()))
            on_zr, on_zi = [
                lax.dot_general(
                    z, jnp.concatenate(before + [half, after], axis=0), dims,
                    precision=highest, preferred_element_type=jnp.float32,
                )
                for half in (z[:k], z[k:])
            ]
            gram = jnp.concatenate([on_zr[:k] + on_zi[k:], on_zi[:k] - on_zr[k:]], axis=0)
            part_ref[step_at + 1, rows_of(c), base:] = gram
            part_ref[step_at + 1, rows_of(c), :spectra] = project(z, real_v, imag_v, k)
        pending += tile_sum(step_at + 1)

    n2 = 2 * k
    stride = tile * cols

    def give(c, d, f):
        peer = lax.rem(me + d, tile)
        lanes = pl.ds(pl.multiple_of(f * stride + me * cols, cols), cols)
        src = give_ref.at[peer, :, c, :, f * cols : (f + 1) * cols]
        dst = out_ref.at[:, c, :, lanes]
        if d == 0:
            return pltpu.make_async_copy(src, dst, own_sem.at[c * freq + f])
        return pltpu.make_async_remote_copy(
            src_ref=src,
            dst_ref=dst,
            send_sem=o_send.at[c, d - 1, f],
            recv_sem=o_recv.at[c, d - 1, f],
            device_id={"tile": peer},
            device_id_type=MESH,
        )

    copies = []
    for c in range(chans):
        m_re, m_im = inverse_factor(sum_ref[ITERS, rows_of(c), base:], k, off)
        w = mix(m_re, m_im, sum_ref[ITERS, rows_of(c), :spectra], k)
        q = mix(m_re, m_im, z_ref[c], k)
        turned = jnp.concatenate([q[k:], -q[:k]], axis=0)
        w3 = split3(w)
        w_left = jnp.concatenate([w3[:n2], w3[:n2], w3[n2 : 2 * n2], w3[n2 : 2 * n2], w3[:n2], w3[2 * n2 :]], axis=0)
        for r, side in ((0, q), (1, turned)):
            s3 = split3(side)
            s_right = jnp.concatenate(
                [s3[:n2], s3[n2 : 2 * n2], s3[:n2], s3[n2 : 2 * n2], s3[2 * n2 :], s3[:n2]], axis=0
            )
            cleaned = v_ref[c, r].astype(jnp.float32) - tn(w_left, s_right)
            give_ref[:, r, c] = cleaned.reshape(tile, block, width).astype(jnp.bfloat16)
        for d in range(tile):
            for f in range(freq):
                copy = give(c, d, f)
                copy.start()
                copies.append(copy)
    for copy in copies:
        copy.wait()
    for copy in pending:
        copy.wait_send()


def channelize_kernel(volts_ref, table_ref, out_ref):
    step = pl.program_id(0)
    span = (STEP + TAPS - 1) * P_SIZE
    start = pl.multiple_of(step * (STEP * P_SIZE), P_SIZE)
    chunk = volts_ref[:, pl.ds(start, span)]
    result = nt(table_ref[...], chunk)
    out_ref[...] = result.reshape(out_ref.shape).astype(jnp.bfloat16)


def channelize(voltages, table, rows, spectra_all):
    inputs_local, samples = voltages.shape
    return pl.pallas_call(
        channelize_kernel,
        grid=(spectra_all // STEP,),
        in_specs=[VMEM, VMEM],
        out_specs=pl.BlockSpec((rows, STEP, inputs_local), lambda i: (0, i, 0)),
        out_shape=jax.ShapeDtypeStruct((rows, spectra_all, inputs_local), jnp.bfloat16),
        compiler_params=pltpu.CompilerParams(vmem_limit_bytes=40 * 2**20),
    )(voltages, table)


def start_kernel(v_ref, q_ref, pg_ref, *, k, lanes):
    chans, _, spectra, _ = v_ref.shape
    pg_ref[...] = jnp.zeros_like(pg_ref)
    for c in range(chans):
        pg_ref[2 * k * c : 2 * k * (c + 1), :spectra] = project(q_ref[...], v_ref[c, 0], v_ref[c, 1], k)


def step_kernel(v_ref, z_ref, pg_ref, z_out, pg_out, *, k, lanes, first):
    chans, _, spectra, width = v_ref.shape
    pg_out[...] = jnp.zeros_like(pg_out)
    for c in range(chans):
        at = slice(2 * k * c, 2 * k * (c + 1))
        weights = pg_ref[at, :spectra]
        basis = z_ref[...] if first else z_ref[c]
        if not first:
            m_re, m_im = inverse_factor(pg_ref[at, lanes:], k)
            weights = mix(m_re, m_im, weights, k)
            basis = mix(m_re, m_im, basis, k)
        real_v, imag_v = v_ref[c, 0], v_ref[c, 1]
        parts = split3(weights / spectra)
        on_re = fold3(plain(parts, real_v))
        on_im = fold3(plain(parts, imag_v))
        z = jnp.concatenate([on_re[:k] - on_im[k:], on_re[k:] + on_im[:k]], axis=0) + loading * basis
        z_out[c] = z
        pg_out[at, :spectra] = project(z, real_v, imag_v, k)
        pad = jnp.zeros((lanes_pad(k), width), jnp.float32)
        right = jnp.concatenate([z[:k], pad], axis=0)
        right_im = jnp.concatenate([z[k:], pad], axis=0)
        dims = (((1,), (1,)), ((), ()))
        first_dot = lax.dot_general(z, right, dims, precision=highest, preferred_element_type=jnp.float32)
        second_dot = lax.dot_general(z, right_im, dims, precision=highest, preferred_element_type=jnp.float32)
        g_re = first_dot[:k] + second_dot[k:]
        g_im = second_dot[:k] - first_dot[k:]
        pg_out[at, lanes:] = jnp.concatenate([g_re, g_im], axis=0)


def lanes_pad(k):
    return 128 - k


def clean_kernel(v_ref, z_ref, pg_ref, out_ref, *, k, lanes):
    chans, _, spectra, width = v_ref.shape
    parts_count, _, _, block, _ = out_ref.shape
    for c in range(chans):
        at = slice(2 * k * c, 2 * k * (c + 1))
        m_re, m_im = inverse_factor(pg_ref[at, lanes:], k)
        w = mix(m_re, m_im, pg_ref[at, :spectra], k)
        q = mix(m_re, m_im, z_ref[c], k)
        turned = jnp.concatenate([q[k:], -q[:k]], axis=0)
        w3 = split3(w)
        n2 = 2 * k
        w_left = jnp.concatenate([w3[:n2], w3[:n2], w3[n2 : 2 * n2], w3[n2 : 2 * n2], w3[:n2], w3[2 * n2 :]], axis=0)
        for r, side in ((0, q), (1, turned)):
            s3 = split3(side)
            s_right = jnp.concatenate(
                [s3[:n2], s3[n2 : 2 * n2], s3[:n2], s3[n2 : 2 * n2], s3[2 * n2 :], s3[:n2]], axis=0
            )
            fitted = tn(w_left, s_right)
            cleaned = v_ref[c, r].astype(jnp.float32) - fitted
            out_ref[:, r, c] = cleaned.reshape(parts_count, block, width).astype(jnp.bfloat16)


def reduce_kernel(x_ref, out_ref, land_ref, send1, recv1, send2, recv2, *, size, chunk):
    me = lax.axis_index("tile")
    barrier = pltpu.get_barrier_semaphore()
    for d in range(1, size):
        peer = lax.rem(me + d, size)
        pl.semaphore_signal(barrier, inc=1, device_id={"tile": peer}, device_id_type=MESH)
    pl.semaphore_wait(barrier, size - 1)
    mine = pl.ds(pl.multiple_of(me * chunk, 8), chunk)
    sends = []
    for d in range(1, size):
        peer = lax.rem(me + d, size)
        copy = pltpu.make_async_remote_copy(
            src_ref=x_ref.at[pl.ds(pl.multiple_of(peer * chunk, 8), chunk)],
            dst_ref=land_ref.at[d - 1],
            send_sem=send1.at[d - 1],
            recv_sem=recv1.at[d - 1],
            device_id={"tile": peer},
            device_id_type=MESH,
        )
        copy.start()
        sends.append(copy)
    total = x_ref[mine]
    for d in range(1, size):
        sends[d - 1].wait_recv()
        total = total + land_ref[d - 1]
    out_ref[mine] = total
    later = []
    for d in range(1, size):
        peer = lax.rem(me + d, size)
        copy = pltpu.make_async_remote_copy(
            src_ref=out_ref.at[mine],
            dst_ref=out_ref.at[mine],
            send_sem=send2.at[d - 1],
            recv_sem=recv2.at[d - 1],
            device_id={"tile": peer},
            device_id_type=MESH,
        )
        copy.start()
        later.append(copy)
    for copy in later:
        copy.wait_recv()
    for copy in sends + later:
        copy.wait_send()


def tile_sum(x, size):
    rows, width = x.shape
    chunk = rows // size
    return pl.pallas_call(
        functools.partial(reduce_kernel, size=size, chunk=chunk),
        in_specs=[VMEM],
        out_specs=VMEM,
        out_shape=jax.ShapeDtypeStruct(x.shape, jnp.float32),
        scratch_shapes=[pltpu.VMEM((size - 1, chunk, width), jnp.float32)]
        + [pltpu.SemaphoreType.DMA((size - 1,))] * 4,
        compiler_params=pltpu.CompilerParams(collective_id=0, has_side_effects=True),
    )(x)


def up(value, unit):
    return -(-value // unit) * unit


def body_split(voltages, channel_ids, start_basis):
    inputs_local, samples_count = voltages.shape
    freq_count = lax.axis_size("freq")
    tile_count = lax.axis_size("tile")
    channels = channel_ids.shape[0]
    chan_local = channels // freq_count
    spectra_all = samples_count // P_SIZE - TAPS + 1
    spectra_local = spectra_all // tile_count
    k = start_basis.shape[1]
    width = freq_count * inputs_local

    coeffs = make_table(channel_ids, TAPS, P_SIZE).reshape(TAPS, 2 * channels, P_SIZE)
    local = channelize(voltages, banded(coeffs), 2 * channels, spectra_all)
    parcel = local.reshape(2, freq_count, chan_local, spectra_all, inputs_local)
    arrived = lax.all_to_all(parcel, "freq", split_axis=1, concat_axis=1, tiled=True)
    values = jnp.transpose(arrived, (2, 0, 3, 1, 4)).reshape(chan_local, 2, spectra_all, width)

    mine = lax.axis_index("tile")
    start = start_basis.reshape(2 * k, freq_count, tile_count, inputs_local)
    start = lax.dynamic_index_in_dim(start, mine, 2, keepdims=False).reshape(2 * k, width)

    lanes = up(spectra_all, 128)
    chunk = up(-(-chan_local * 2 * k // tile_count), 8)
    packed = jax.ShapeDtypeStruct((tile_count * chunk, lanes + 128), jnp.float32)
    z_shape = jax.ShapeDtypeStruct((chan_local, 2 * k, width), jnp.float32)
    params = pltpu.CompilerParams(vmem_limit_bytes=40 * 2**20)

    partial = pl.pallas_call(
        functools.partial(start_kernel, k=k, lanes=lanes),
        in_specs=[VMEM] * 2, out_specs=VMEM, out_shape=packed, compiler_params=params,
    )(values, start)
    z = start
    for step_at in range(ITERS):
        total = tile_sum(partial, tile_count)
        z, partial = pl.pallas_call(
            functools.partial(step_kernel, k=k, lanes=lanes, first=step_at == 0),
            in_specs=[VMEM] * 3, out_specs=[VMEM] * 2, out_shape=[z_shape, packed],
            compiler_params=params,
        )(values, z, total)
    total = tile_sum(partial, tile_count)
    cleaned = pl.pallas_call(
        functools.partial(clean_kernel, k=k, lanes=lanes),
        in_specs=[VMEM] * 3, out_specs=VMEM,
        out_shape=jax.ShapeDtypeStruct((tile_count, 2, chan_local, spectra_local, width), jnp.bfloat16),
        compiler_params=params,
    )(values, z, total)
    moved = lax.all_to_all(cleaned, "tile", split_axis=0, concat_axis=0, tiled=True)
    moved = moved.reshape(tile_count, 2, chan_local, spectra_local, freq_count, inputs_local)
    moved = jnp.transpose(moved, (1, 2, 3, 4, 0, 5)).astype(jnp.float32)
    return moved.reshape(2, chan_local, spectra_local, freq_count * tile_count * inputs_local)


def body(voltages, channel_ids, start_basis):
    inputs_local, samples_count = voltages.shape
    freq_count = lax.axis_size("freq")
    tile_count = lax.axis_size("tile")
    if inputs_local % 128:
        return body_split(voltages, channel_ids, start_basis)
    channels = channel_ids.shape[0]
    chan_local = channels // freq_count
    spectra_all = samples_count // P_SIZE - TAPS + 1
    spectra_local = spectra_all // tile_count
    k = start_basis.shape[1]
    width = freq_count * inputs_local

    coeffs = make_table(channel_ids, TAPS, P_SIZE)
    coeffs = coeffs.reshape(TAPS, 2, channels, P_SIZE).transpose(0, 2, 1, 3).reshape(TAPS, 2 * channels, P_SIZE)
    mine = lax.axis_index("tile")
    start = start_basis.reshape(2 * k, freq_count, tile_count, inputs_local)
    start = lax.dynamic_index_in_dim(start, mine, 2, keepdims=False).reshape(2 * k, width)

    base, off = spectra_all // 128 * 128, spectra_all % 128
    if off + k > 128:
        base, off = base + 128, 0
    rows = tile_count * up(-(-chan_local * 2 * k // tile_count), 8)
    chunk = rows // tile_count
    rounds = ITERS + 1
    peers = tile_count - 1
    steps = spectra_all // STEP
    sem = pltpu.SemaphoreType.DMA
    cleaned = pl.pallas_call(
        functools.partial(fused_kernel, k=k, freq=freq_count, tile=tile_count, base=base, off=off),
        in_specs=[VMEM] * 3,
        out_specs=VMEM,
        out_shape=jax.ShapeDtypeStruct(
            (2, chan_local, spectra_local, width * tile_count), jnp.bfloat16
        ),
        scratch_shapes=[
            pltpu.VMEM((freq_count, chan_local, 2, spectra_all, inputs_local), jnp.bfloat16),
            pltpu.VMEM((chan_local, 2, spectra_all, width), jnp.bfloat16),
            pltpu.VMEM((chan_local, 2 * k, width), jnp.float32),
            pltpu.VMEM((rounds, rows, base + 128), jnp.float32),
            pltpu.VMEM((rounds, peers, chunk, base + 128), jnp.float32),
            pltpu.VMEM((rounds, rows, base + 128), jnp.float32),
            pltpu.VMEM((tile_count, 2, chan_local, spectra_local, width), jnp.bfloat16),
            sem((steps, freq_count - 1)), sem((steps, freq_count - 1)),
            sem((rounds, peers)), sem((rounds, peers)),
            sem((rounds, peers)), sem((rounds, peers)),
            sem((chan_local, peers, freq_count)), sem((chan_local, peers, freq_count)),
            sem((max(steps, chan_local * freq_count),)),
        ],
        compiler_params=pltpu.CompilerParams(
            collective_id=0, has_side_effects=True, vmem_limit_bytes=56 * 2**20
        ),
    )(voltages, banded(coeffs), start)
    return cleaned.astype(jnp.float32)


def solution(mesh):
    in_specs = (P(("freq", "tile"), None), P(), P())
    out_specs = P(None, "freq", "tile", None)
    return jax.shard_map(body, mesh=mesh, in_specs=in_specs, out_specs=out_specs, check_vma=False)
```

profile of v0, /device:TPU:0, one launch (start us, length us, event | category | flops | bytes accessed | tf_op | source)
XLA Modules:
  0.0 101.7 jit_solution(9264399535677831279)
XLA Ops:
  0.0 0.9 fusion.7
  1.0 0.7 fusion.41
  2.3 0.1 fusion.17
  2.4 0.9 select_select_fusion
  3.3 0.0 copy-start
  3.3 1.5 %copy.12 = bf16[48,8,19,128]{3,1,2,0:T(8,128)(2,1)} copy(bf16[48,8,19,128]{3,2,1,0:T(8,128)(2,1)S(1)} %bitcast.22) | data formatting | bytes 3735552
  4.8 0.0 copy-done
  4.8 0.1 copy.8
  4.9 0.6 copy.13
  5.5 93.3 %shard_map.37 = bf16[2,3,24,4096]{3,2,1,0:T(8,128)(2,1)} custom-call(bf16[128,24960]{1,0:T(8,128)(2,1)} %volts_ref.1, bf16[384,2432]{1,0:T(8,128)(2,1)} %bitcast.23, f32[16,512]{1,0:T(8,128)} %bitcast.26), custom_call_target="tpu_custom_call" | custom-call | tf_op jit(solution)/shard_map/pallas_call | solution.py:519
  98.8 2.9 %convert_element_type.28 = f32[2,3,24,4096]{3,2,1,0:T(8,128)} convert(bf16[2,3,24,4096]{3,2,1,0:T(8,128)(2,1)} %shard_map.37) | non-fusion elementwise | flops 589824 | bytes 3538944 | tf_op jit(solution)/shard_map/convert_element_type | solution.py:544
  (6 shorter events, 0.1 us)
Async XLA Ops:
  3.3 1.5 %copy-start = (f32[2,8,4096]{2,1,0:T(8,128)S(1)}, f32[2,8,4096]{2,1,0:T(8,128)}, u32[]{:S(2)}) copy-start(f32[2,8,4096]{2,1,0:T(8,128)} %param.5) | copy-start | bytes 786436
where the time goes:
time: 102 us
  Pallas kernels  93.3 us (91%)
  other arithmetic  5.49 us (5%)
  local copies, waits for them, and re-layouts  2.22 us (2%)
    pallas_call x1, Pallas kernels, body(): pl.pallas_call(functools.partial(fused_kernel, k=k, freq=freq_count, tile...  93.3 us
    convert_element_type x1, other arithmetic, body(): return cleaned.astype(jnp.float32)  2.93 us
    unnamed x5, local copies, waits for them, and re-layouts  2.17 us

commit v1 on v0

--- a/solution.py
+++ b/solution.py
@@ -12,6 +12,8 @@
 P_SIZE = 128
 ITERS = 3
 STEP = 16
+SUB = 8
+LAG = 4
 
 loading = 0.5
 highest = lax.Precision.HIGHEST
@@ -112,182 +114,445 @@
 
 
 def fused_kernel(
-    volts_ref, table_ref, start_ref, out_ref,
-    stage, v_ref, z_ref, part_ref, land_ref, sum_ref, give_ref,
-    f_send, f_recv, r_send, r_recv, g_send, g_recv, o_send, o_recv, own_sem,
-    *, k, freq, tile, base, off,
+    volts_hbm, ids_ref, start_ref, own_ref, q_ref, left_ref,
+    vol_ref, table_ref, stage, v_ref, parts_ref, pack_ref, pair_ref, half_ref, land_ref, full_ref, res_ref,
+    vol_sem, own_sem, mine_sem, f_send, f_recv, z_send, z_recv,
+    p_send, p_recv, k_send, k_recv, j_send, j_recv, b_send, b_recv,
+    up_send, down_send, line_recv, mate_send, mate_recv,
+    *, k, freq, tile,
 ):
-    chans, _, spectra, width = v_ref.shape
-    cols = volts_ref.shape[0]
-    steps = spectra // STEP
+    chans, _, spectra, width = parts_ref.shape
+    cols = vol_ref.shape[1]
     block = spectra // tile
-    chunk = part_ref.shape[1] // tile
+    rows = 2 * block
+    subs = block // SUB
+    window = vol_ref.shape[2]
     group = lax.axis_index("freq")
     me = lax.axis_index("tile")
+    line = tile // 2
+    z, core = me // 2, lax.rem(me, 2)
+    mate = me + 1 - 2 * core
     barrier = pltpu.get_barrier_semaphore()
     for d in range(1, freq):
         pl.semaphore_signal(barrier, inc=1, device_id={"freq": lax.rem(group + d, freq)}, device_id_type=MESH)
     for d in range(1, tile):
         pl.semaphore_signal(barrier, inc=1, device_id={"tile": lax.rem(me + d, tile)}, device_id_type=MESH)
+
+    def remote(src, dst, send, recv, where):
+        return pltpu.make_async_remote_copy(
+            src_ref=src, dst_ref=dst, send_sem=send, recv_sem=recv, device_id=where, device_id_type=MESH
+        )
+
+    def block_at(j):
+        return lax.rem(j, 2) * (tile // 2) + j // 2
+
+    def fetch(j):
+        lanes = pl.ds(pl.multiple_of(block_at(j) * (block * P_SIZE), P_SIZE), window)
+        return pltpu.make_async_copy(volts_hbm.at[:, lanes], vol_ref.at[j], vol_sem.at[j])
+
+    for j in range(tile):
+        fetch(j).start()
+
+    build_table(ids_ref, table_ref)
     pl.semaphore_wait(barrier, freq - 1 + tile - 1)
 
-    span = (STEP + TAPS - 1) * P_SIZE
+    def rows_of(b):
+        return pl.ds(pl.multiple_of(b * rows, rows), rows)
+
     my_cols = pl.ds(pl.multiple_of(group * cols, cols), cols)
 
-    def handover(i, d):
+    def handover(j, d):
         peer = lax.rem(group + d, freq)
-        rows = pl.ds(pl.multiple_of(i * STEP, STEP), STEP)
-        return pltpu.make_async_remote_copy(
-            src_ref=stage.at[peer, :, :, rows, :],
-            dst_ref=v_ref.at[:, :, rows, my_cols],
-            send_sem=f_send.at[i, d - 1],
-            recv_sem=f_recv.at[i, d - 1],
-            device_id={"freq": peer},
-            device_id_type=MESH,
-        )
-
-    def own_part(i):
-        rows = pl.ds(pl.multiple_of(i * STEP, STEP), STEP)
+        return remote(
+            stage.at[j, peer], v_ref.at[:, rows_of(block_at(j)), my_cols],
+            f_send.at[j, d - 1], f_recv.at[j, d - 1], {"freq": peer},
+        )
+
+    def own_part(j):
         return pltpu.make_async_copy(
-            stage.at[group, :, :, rows, :], v_ref.at[:, :, rows, my_cols], own_sem.at[i]
-        )
-
-    def filter_step(i, carry):
-        start = pl.multiple_of(i * (STEP * P_SIZE), P_SIZE)
-        result = nt(table_ref[...], volts_ref[:, pl.ds(start, span)])
-        rows = pl.ds(pl.multiple_of(i * STEP, STEP), STEP)
-        stage[:, :, :, rows, :] = result.reshape(freq, chans, 2, STEP, cols).astype(jnp.bfloat16)
+            stage.at[j, group], v_ref.at[:, rows_of(block_at(j)), my_cols], own_sem.at[j]
+        )
+
+    def filter_step(j):
+        fetch(j).wait()
+        span = (SUB + TAPS - 1) * P_SIZE
+        right = jnp.concatenate(
+            [vol_ref[j, :, n * SUB * P_SIZE : n * SUB * P_SIZE + span] for n in range(subs)], axis=0
+        )
+        result = nt(table_ref[...], right)
+        pieces = [result[:, n * cols : (n + 1) * cols].reshape(-1, SUB, cols) for n in range(subs)]
+        result = jnp.concatenate(pieces, axis=1)
+        stage[j] = result.reshape(freq, chans, rows, cols).astype(jnp.bfloat16)
         for d in range(1, freq):
-            handover(i, d).start()
-        own_part(i).start()
+            handover(j, d).start()
+        own_part(j).start()
+
+    def arrive(j):
+        for d in range(1, freq):
+            handover(j, d).wait_recv()
+        own_part(j).wait()
+
+    def forward(b):
+        return remote(v_ref.at[:, rows_of(b), :], own_ref.at[me], z_send.at[b], z_recv.at[me], {"tile": b})
+
+    def keep(b):
+        return pltpu.make_async_copy(v_ref.at[:, rows_of(b), :], own_ref.at[me], mine_sem)
+
+    def pass_on(j):
+        b = block_at(j)
+
+        @pl.when(b != me)
+        def _():
+            forward(b).start()
+
+        @pl.when(b == me)
+        def _():
+            keep(b).start()
+
+    def first(j, carry):
+        filter_step(j)
         return carry
 
-    lax.fori_loop(0, steps, filter_step, 0)
-
-    def filter_wait(i, carry):
+    def both(j, carry):
+        filter_step(j)
+        arrive(j - LAG)
+        pass_on(j - LAG)
+        return carry
+
+    def last(j, carry):
+        arrive(j)
+        return carry
+
+    lax.fori_loop(0, LAG, first, 0)
+    lax.fori_loop(LAG, tile, both, 0)
+    lax.fori_loop(tile - LAG, tile, last, 0)
+
+    start = jnp.concatenate(
+        [
+            start_ref[:, pl.ds(pl.multiple_of(f * (tile * cols) + me * cols, cols), cols)]
+            for f in range(freq)
+        ],
+        axis=1,
+    )
+    start3 = split3(start)
+    fold = spectra - 128
+    half = pack_ref.shape[2]
+    keep_mask = lax.broadcasted_iota(jnp.int32, (spectra, spectra), 0) >= lax.broadcasted_iota(
+        jnp.int32, (spectra, spectra), 1
+    )
+    pad_lanes = 128 - fold
+
+    def folded(value):
+        count = value.shape[0] // 2
+        wide = jnp.concatenate([value[:, 128:], jnp.zeros((2 * count, pad_lanes), jnp.float32)], axis=1)
+        return wide[:count] + pltpu.roll(wide[count:], fold, 1)
+
+    def to_mate(c):
+        return remote(pack_ref.at[c, 1 - core], pair_ref.at[c], p_send.at[c], p_recv.at[c], {"tile": mate})
+
+    for c in range(chans):
+        loose = v_ref[c].astype(jnp.float32).reshape(tile, 2, block, width)
+        real_v = loose[:, 0].reshape(spectra, width).astype(jnp.bfloat16)
+        imag_v = loose[:, 1].reshape(spectra, width).astype(jnp.bfloat16)
+        parts_ref[c, 0] = real_v
+        parts_ref[c, 1] = imag_v
+        k_re = nt(real_v, real_v) + nt(imag_v, imag_v)
+        k_im = nt(real_v, imag_v) - nt(imag_v, real_v)
+        packed = jnp.where(keep_mask, k_re, k_im)
+        on_re = fold3(nt(start3, real_v))
+        on_im = fold3(nt(start3, imag_v))
+        w = jnp.concatenate([on_re[:k] + on_im[k:], on_re[k:] - on_im[:k]], axis=0)
+        tail = 2 * half - (spectra + spectra // 2 + 3 * k)
+        everything = jnp.concatenate(
+            [packed[:, :128], folded(packed), w[:, :128], folded(w), jnp.zeros((tail, 128), jnp.float32)], axis=0
+        )
+        pack_ref[c] = everything.reshape(2, half, 128)
+        to_mate(c).start()
+
+    def root_line(c):
+        return line // 2 - 1 + c % 2
+
+    def to_root(c, d):
+        return remote(
+            half_ref.at[c], land_ref.at[c, d - 1], k_send.at[c], k_recv.at[c, d - 1],
+            {"tile": 2 * root_line(c) + core},
+        )
+
+    for c in range(chans):
+        to_mate(c).wait_recv()
+        half_ref[c] = pack_ref[c, core] + pair_ref[c]
+        for d in range(1, line):
+
+            @pl.when(z == (root_line(c) + d) % line)
+            def _():
+                to_root(c, d).start()
+
+    for j in range(tile - LAG, tile):
+        pass_on(j)
+
+    g_re = exact(start_ref[...], start_ref[:k])
+    g_im = exact(start_ref[...], start_ref[k:])
+    gram0 = jnp.concatenate([g_re[:k] + g_im[k:], g_im[:k] - g_re[k:]], axis=0)
+
+    def join(c):
+        return remote(half_ref.at[c], full_ref.at[core], j_send.at[c], j_recv.at[c], {"tile": mate})
+
+    for c in range(chans):
+
+        @pl.when(z == root_line(c))
+        def _():
+            total = half_ref[c]
+            for d in range(1, line):
+                to_root(c, d).wait_recv()
+                total = total + land_ref[c, d - 1]
+
+            @pl.when(core == c // 2)
+            def _():
+                full_ref[core] = total
+
+            @pl.when(core != c // 2)
+            def _():
+                half_ref[c] = total
+                join(c).start()
+
+    side = z - (line // 2 - 1)
+    at = side + 2 * core
+    is_root = (side >= 0) & (side < 2) & (at < chans)
+
+    def spread(c, d):
+        return remote(
+            res_ref.at[c], res_ref.at[c], b_send.at[d - 1], b_recv.at[c], {"tile": lax.rem(me + d, tile)}
+        )
+
+    @pl.when(is_root)
+    def _():
+        for c in range(chans):
+
+            @pl.when(at == c)
+            def _():
+                join(c).wait_recv()
+
+        res_ref[at] = iterate(full_ref[...].reshape(2 * half, 128), gram0, k, spectra)
+        for d in range(1, tile):
+            spread(at, d).start()
+
+    def line_copy(c, origin, to, sem):
+        slot = 2 * origin + core
+        return remote(
+            q_ref.at[slot, c], q_ref.at[slot, c], sem.at[c, origin], line_recv.at[c, origin], {"tile": 2 * to + core}
+        )
+
+    def mate_copy(c, origin):
+        slot = 2 * origin + core
+        return remote(
+            q_ref.at[slot, c], q_ref.at[slot, c], mate_send.at[c, origin], mate_recv.at[c, origin], {"tile": mate}
+        )
+
+    def send_on(c, origin, up, down):
+        if up:
+
+            @pl.when(z < line - 1)
+            def _():
+                line_copy(c, origin, z + 1, up_send).start()
+
+        if down:
+
+            @pl.when(z > 0)
+            def _():
+                line_copy(c, origin, z - 1, down_send).start()
+
+        mate_copy(c, origin).start()
+
+    for c in range(chans):
+
+        @pl.when(jnp.logical_not(is_root & (at == c)))
+        def _():
+            spread(c, 1).wait_recv()
+
+        w = res_ref[c, :, :spectra]
+        a = res_ref[c, :, 256 : 256 + spectra]
+        b = res_ref[c, :, 512:640]
+        parts = split3(a)
+        on_re = fold3(plain(parts, parts_ref[c, 0]))
+        on_im = fold3(plain(parts, parts_ref[c, 1]))
+        q = jnp.concatenate([on_re[:k] - on_im[k:], on_re[k:] + on_im[:k]], axis=0)
+        q_ref[me, c] = q + mix(b[:k], b[k:], start, k)
+        send_on(c, z, True, True)
+        turned = jnp.concatenate([-w[k:], w[:k]], axis=0)
+        chosen = jnp.zeros((2 * k, rows), jnp.float32)
+        for t in range(tile):
+            lanes = slice(t * block, (t + 1) * block)
+            pair = jnp.concatenate([w[:, lanes], turned[:, lanes]], axis=1)
+            chosen = jnp.where(me == t, pair, chosen)
+        left_ref[c] = chosen
+
+    for d in range(1, line):
+        for c in range(chans):
+
+            @pl.when(z >= d)
+            def _():
+                line_copy(c, z - d, z, up_send).wait_recv()
+                send_on(c, z - d, True, False)
+
+            @pl.when(z + d < line)
+            def _():
+                line_copy(c, z + d, z, down_send).wait_recv()
+                send_on(c, z + d, False, True)
+
+    for c in range(chans):
+        for origin in range(line):
+            mate_copy(c, origin).wait()
+
+            @pl.when((z >= origin) & (z < line - 1))
+            def _():
+                line_copy(c, origin, z + 1, up_send).wait_send()
+
+            @pl.when((z <= origin) & (z > 0))
+            def _():
+                line_copy(c, origin, z - 1, down_send).wait_send()
+
+    def drain(j, carry):
         for d in range(1, freq):
-            handover(i, d).wait()
-        own_part(i).wait()
+            handover(j, d).wait_send()
+
+        @pl.when(j != me)
+        def _():
+            forward(j).wait_send()
+            remote(v_ref.at[:, rows_of(j), :], own_ref.at[j], z_send.at[j], z_recv.at[j], {"tile": j}).wait_recv()
+
+        @pl.when(j == me)
+        def _():
+            keep(j).wait()
+
         return carry
 
-    lax.fori_loop(0, steps, filter_wait, 0)
-
-    mine = pl.ds(pl.multiple_of(me * chunk, 8), chunk)
-
-    def tile_sum(at):
-        sends = []
+    lax.fori_loop(0, tile, drain, 0)
+    for c in range(chans):
+        to_mate(c).wait_send()
+
+        @pl.when(z != root_line(c))
+        def _():
+            to_root(c, 1).wait_send()
+
+        @pl.when((z == root_line(c)) & (core != c // 2))
+        def _():
+            join(c).wait_send()
+
+    @pl.when(is_root)
+    def _():
         for d in range(1, tile):
-            peer = lax.rem(me + d, tile)
-            copy = pltpu.make_async_remote_copy(
-                src_ref=part_ref.at[at, pl.ds(pl.multiple_of(peer * chunk, 8), chunk)],
-                dst_ref=land_ref.at[at, d - 1],
-                send_sem=r_send.at[at, d - 1],
-                recv_sem=r_recv.at[at, d - 1],
-                device_id={"tile": peer},
-                device_id_type=MESH,
-            )
-            copy.start()
-            sends.append(copy)
-        total = part_ref[at, mine]
-        for d in range(1, tile):
-            sends[d - 1].wait_recv()
-            total = total + land_ref[at, d - 1]
-        sum_ref[at, mine] = total
-        for d in range(1, tile):
-            copy = pltpu.make_async_remote_copy(
-                src_ref=sum_ref.at[at, mine],
-                dst_ref=sum_ref.at[at, mine],
-                send_sem=g_send.at[at, d - 1],
-                recv_sem=g_recv.at[at, d - 1],
-                device_id={"tile": lax.rem(me + d, tile)},
-                device_id_type=MESH,
-            )
-            copy.start()
-            sends.append(copy)
-        for copy in sends[tile - 1 :]:
-            copy.wait_recv()
-        return sends
-
-    def rows_of(c):
-        return slice(2 * k * c, 2 * k * (c + 1))
-
-    part_ref[...] = jnp.zeros_like(part_ref)
-    for c in range(chans):
-        part_ref[0, rows_of(c), :spectra] = project(start_ref[...], v_ref[c, 0], v_ref[c, 1], k)
-    pending = tile_sum(0)
-    for step_at in range(ITERS):
-        for c in range(chans):
-            weights = sum_ref[step_at, rows_of(c), :spectra]
-            if step_at == 0:
-                basis = start_ref[...]
-            else:
-                m_re, m_im = inverse_factor(sum_ref[step_at, rows_of(c), base:], k, off)
-                weights = mix(m_re, m_im, weights, k)
-                basis = mix(m_re, m_im, z_ref[c], k)
-            real_v, imag_v = v_ref[c, 0], v_ref[c, 1]
-            parts = split3(weights / spectra)
-            on_re = fold3(plain(parts, real_v))
-            on_im = fold3(plain(parts, imag_v))
-            z = jnp.concatenate([on_re[:k] - on_im[k:], on_re[k:] + on_im[:k]], axis=0) + loading * basis
-            z_ref[c] = z
-            before = [jnp.zeros((off, width), jnp.float32)] if off else []
-            after = jnp.zeros((128 - off - k, width), jnp.float32)
-            dims = (((1,), (1,)), ((), ()))
-            on_zr, on_zi = [
-                lax.dot_general(
-                    z, jnp.concatenate(before + [half, after], axis=0), dims,
-                    precision=highest, preferred_element_type=jnp.float32,
-                )
-                for half in (z[:k], z[k:])
-            ]
-            gram = jnp.concatenate([on_zr[:k] + on_zi[k:], on_zi[:k] - on_zr[k:]], axis=0)
-            part_ref[step_at + 1, rows_of(c), base:] = gram
-            part_ref[step_at + 1, rows_of(c), :spectra] = project(z, real_v, imag_v, k)
-        pending += tile_sum(step_at + 1)
-
+            spread(at, d).wait_send()
+
+
+def exact(left, right):
+    return lax.dot_general(
+        left, right, (((1,), (1,)), ((), ())), precision=highest, preferred_element_type=jnp.float32
+    )
+
+
+def build_table(ids_ref, table_ref):
+    count = ids_ref.shape[0]
+    length = TAPS * P_SIZE
+    tap = lax.broadcasted_iota(jnp.int32, (8, P_SIZE), 0)
+    point = lax.broadcasted_iota(jnp.int32, (8, P_SIZE), 1)
+    offsets = (tap * P_SIZE + point).astype(jnp.float32)
+    shifted = math.pi * ((offsets + 0.5 - length / 2.0) / P_SIZE)
+    shape = jnp.sin(shifted) / shifted
+    shape = shape * (0.5 - 0.5 * jnp.cos(2.0 * math.pi * (offsets + 0.5) / length))
+    shape = jnp.where(tap < TAPS, shape, 0.0)
+    total = jnp.sum(jnp.sum(shape * shape, axis=1, keepdims=True), axis=0, keepdims=True)
+    shape = shape / jnp.sqrt(total)
+    part = lax.broadcasted_iota(jnp.int32, (count, P_SIZE), 0)
+    place = lax.broadcasted_iota(jnp.int32, (count, P_SIZE), 1)
+    phases = jnp.bitwise_and(ids_ref[...] * place, P_SIZE - 1)
+    angles = 2.0 * math.pi / P_SIZE * phases.astype(jnp.float32)
+    rotors = jnp.where(jnp.bitwise_and(part, 1) == 0, jnp.cos(angles), -jnp.sin(angles))
+    spread = []
+    for m in range(TAPS):
+        taps = rotors * shape[m : m + 1]
+        spread.append(jnp.broadcast_to(taps[:, None, :], (count, SUB, P_SIZE)))
+    at = lax.broadcasted_iota(jnp.int32, (count, SUB, P_SIZE), 1)
+    for frame in range(SUB + TAPS - 1):
+        value = jnp.zeros((count, SUB, P_SIZE), jnp.float32)
+        for m in range(TAPS):
+            if 0 <= frame - m < SUB:
+                value = jnp.where(at == frame - m, spread[m], value)
+        table_ref[:, frame * P_SIZE : (frame + 1) * P_SIZE] = value.reshape(count * SUB, P_SIZE).astype(jnp.bfloat16)
+
+
+def iterate(full, gram0, k, spectra):
+    fold = spectra - 128
+    count = spectra // 2
+    lane = lax.broadcasted_iota(jnp.int32, (1, 128), 1)
+
+    def unfold(top, bent):
+        low = jnp.where(lane < fold, bent, 0.0)
+        high = jnp.where(lane < fold, pltpu.roll(bent, 128 - fold, 1), 0.0)
+        return jnp.concatenate([top, jnp.concatenate([low, high], axis=0)], axis=1)
+
+    packed = unfold(full[:spectra], full[spectra : spectra + count])
+    at = spectra + count
+    w = unfold(full[at : at + 2 * k], full[at + 2 * k : at + 3 * k])
+    packed = jnp.concatenate([packed, jnp.zeros((256 - spectra, 256), jnp.float32)], axis=0)
+    turned = packed.T
+    row = lax.broadcasted_iota(jnp.int32, (256, 256), 0)
+    col = lax.broadcasted_iota(jnp.int32, (256, 256), 1)
+    k_re = jnp.where(row >= col, packed, turned)
+    k_im = jnp.where(row < col, packed, jnp.where(row > col, -turned, 0.0))
+    both = jnp.concatenate([k_re, k_im], axis=1)
+    high = both.astype(jnp.bfloat16)
+    rest = both - high.astype(jnp.float32)
+    mid = rest.astype(jnp.bfloat16)
+    low = (rest - mid.astype(jnp.float32)).astype(jnp.bfloat16)
     n2 = 2 * k
-    stride = tile * cols
-
-    def give(c, d, f):
-        peer = lax.rem(me + d, tile)
-        lanes = pl.ds(pl.multiple_of(f * stride + me * cols, cols), cols)
-        src = give_ref.at[peer, :, c, :, f * cols : (f + 1) * cols]
-        dst = out_ref.at[:, c, :, lanes]
-        if d == 0:
-            return pltpu.make_async_copy(src, dst, own_sem.at[c * freq + f])
-        return pltpu.make_async_remote_copy(
-            src_ref=src,
-            dst_ref=dst,
-            send_sem=o_send.at[c, d - 1, f],
-            recv_sem=o_recv.at[c, d - 1, f],
-            device_id={"tile": peer},
-            device_id_type=MESH,
-        )
-
-    copies = []
-    for c in range(chans):
-        m_re, m_im = inverse_factor(sum_ref[ITERS, rows_of(c), base:], k, off)
-        w = mix(m_re, m_im, sum_ref[ITERS, rows_of(c), :spectra], k)
-        q = mix(m_re, m_im, z_ref[c], k)
-        turned = jnp.concatenate([q[k:], -q[:k]], axis=0)
+    a = jnp.zeros((n2, 256), jnp.float32)
+    b = jnp.where(
+        lax.broadcasted_iota(jnp.int32, (n2, 128), 0) == lax.broadcasted_iota(jnp.int32, (n2, 128), 1), 1.0, 0.0
+    )
+    b = jnp.where(lax.broadcasted_iota(jnp.int32, (n2, 128), 0) < k, b, 0.0)
+    held = gram0
+    for _ in range(ITERS):
         w3 = split3(w)
+        on_high = plain(w3, high)
+        on_mid = plain(w3[: 2 * n2], mid)
+        on_low = plain(w3[:n2], low)
+        kw = (on_low + on_mid[n2:] + on_high[2 * n2 :]) + (on_mid[:n2] + on_high[n2 : 2 * n2]) + on_high[:n2]
+        on_re, on_im = kw[:, :256], kw[:, 256:]
+        kw = jnp.concatenate([on_re[:k] + on_im[k:], on_re[k:] - on_im[:k]], axis=0)
+        y = kw / spectra + loading * w
+        u = (y + loading * w) / spectra
+        g_re = exact(w, u[:k])
+        g_im = exact(w, u[k:])
+        gram = jnp.concatenate([g_re[:k] + g_im[k:], g_im[:k] - g_re[k:]], axis=0) + loading * loading * held
+        m_re, m_im = inverse_factor(gram, k)
+        grown = jnp.concatenate([y, w / spectra + loading * a, loading * b], axis=1)
+        grown = mix(m_re, m_im, grown, k)
+        w, a, b = grown[:, :256], grown[:, 256:512], grown[:, 512:]
+        held = b_identity(n2, k)
+    return jnp.concatenate([w, a, b], axis=1)
+
+
+def b_identity(n2, k):
+    row = lax.broadcasted_iota(jnp.int32, (n2, k), 0)
+    col = lax.broadcasted_iota(jnp.int32, (n2, k), 1)
+    return jnp.where(row == col, 1.0, 0.0)
+
+
+def finish_kernel(own_ref, q_ref, left_ref, out_ref):
+    tile, chans, rows, cols = own_ref.shape
+    block = rows // 2
+    n2 = q_ref.shape[2]
+    for c in range(chans):
+        w3 = split3(left_ref[c])
         w_left = jnp.concatenate([w3[:n2], w3[:n2], w3[n2 : 2 * n2], w3[n2 : 2 * n2], w3[:n2], w3[2 * n2 :]], axis=0)
-        for r, side in ((0, q), (1, turned)):
-            s3 = split3(side)
+        for t in range(tile):
+            s3 = split3(q_ref[t, c])
             s_right = jnp.concatenate(
                 [s3[:n2], s3[n2 : 2 * n2], s3[:n2], s3[n2 : 2 * n2], s3[2 * n2 :], s3[:n2]], axis=0
             )
-            cleaned = v_ref[c, r].astype(jnp.float32) - tn(w_left, s_right)
-            give_ref[:, r, c] = cleaned.reshape(tile, block, width).astype(jnp.bfloat16)
-        for d in range(tile):
-            for f in range(freq):
-                copy = give(c, d, f)
-                copy.start()
-                copies.append(copy)
-    for copy in copies:
-        copy.wait()
-    for copy in pending:
-        copy.wait_send()
+            cleaned = own_ref[t, c].astype(jnp.float32) - tn(w_left, s_right)
+            out_ref[0, c, :, t * cols : (t + 1) * cols] = cleaned[:block]
+            out_ref[1, c, :, t * cols : (t + 1) * cols] = cleaned[block:]
 
 
 def channelize_kernel(volts_ref, table_ref, out_ref):
@@ -500,48 +765,64 @@
     spectra_local = spectra_all // tile_count
     k = start_basis.shape[1]
     width = freq_count * inputs_local
-
-    coeffs = make_table(channel_ids, TAPS, P_SIZE)
-    coeffs = coeffs.reshape(TAPS, 2, channels, P_SIZE).transpose(0, 2, 1, 3).reshape(TAPS, 2 * channels, P_SIZE)
-    mine = lax.axis_index("tile")
-    start = start_basis.reshape(2 * k, freq_count, tile_count, inputs_local)
-    start = lax.dynamic_index_in_dim(start, mine, 2, keepdims=False).reshape(2 * k, width)
-
-    base, off = spectra_all // 128 * 128, spectra_all % 128
-    if off + k > 128:
-        base, off = base + 128, 0
-    rows = tile_count * up(-(-chan_local * 2 * k // tile_count), 8)
-    chunk = rows // tile_count
-    rounds = ITERS + 1
-    peers = tile_count - 1
-    steps = spectra_all // STEP
+    if spectra_all != 192 or spectra_local % SUB or tile_count % 4 or chan_local > 4 or k != 8:
+        return body_split(voltages, channel_ids, start_basis)
+
+    ids = jnp.broadcast_to(jnp.repeat(channel_ids, 2)[:, None], (2 * channels, P_SIZE))
+    start = start_basis.reshape(2 * k, freq_count * tile_count * inputs_local)
+    rows = 2 * spectra_local
+    line = tile_count // 2
+    half = up(spectra_all + spectra_all // 2 + 3 * k, 16) // 2
     sem = pltpu.SemaphoreType.DMA
-    cleaned = pl.pallas_call(
-        functools.partial(fused_kernel, k=k, freq=freq_count, tile=tile_count, base=base, off=off),
-        in_specs=[VMEM] * 3,
-        out_specs=VMEM,
-        out_shape=jax.ShapeDtypeStruct(
-            (2, chan_local, spectra_local, width * tile_count), jnp.bfloat16
-        ),
+    peers = freq_count - 1
+    own, q, left = pl.pallas_call(
+        functools.partial(fused_kernel, k=k, freq=freq_count, tile=tile_count),
+        in_specs=[pl.BlockSpec(memory_space=pl.ANY), VMEM, VMEM],
+        out_specs=[pl.BlockSpec(memory_space=pl.ANY), VMEM, VMEM],
+        out_shape=[
+            jax.ShapeDtypeStruct((tile_count, chan_local, rows, width), jnp.bfloat16),
+            jax.ShapeDtypeStruct((tile_count, chan_local, 2 * k, width), jnp.float32),
+            jax.ShapeDtypeStruct((chan_local, 2 * k, rows), jnp.float32),
+        ],
         scratch_shapes=[
-            pltpu.VMEM((freq_count, chan_local, 2, spectra_all, inputs_local), jnp.bfloat16),
+            pltpu.VMEM((tile_count, inputs_local, (spectra_local + TAPS - 1) * P_SIZE), jnp.bfloat16),
+            pltpu.VMEM((2 * channels * SUB, (SUB + TAPS - 1) * P_SIZE), jnp.bfloat16),
+            pltpu.VMEM((tile_count, freq_count, chan_local, rows, inputs_local), jnp.bfloat16),
+            pltpu.VMEM((chan_local, tile_count * rows, width), jnp.bfloat16),
             pltpu.VMEM((chan_local, 2, spectra_all, width), jnp.bfloat16),
-            pltpu.VMEM((chan_local, 2 * k, width), jnp.float32),
-            pltpu.VMEM((rounds, rows, base + 128), jnp.float32),
-            pltpu.VMEM((rounds, peers, chunk, base + 128), jnp.float32),
-            pltpu.VMEM((rounds, rows, base + 128), jnp.float32),
-            pltpu.VMEM((tile_count, 2, chan_local, spectra_local, width), jnp.bfloat16),
-            sem((steps, freq_count - 1)), sem((steps, freq_count - 1)),
-            sem((rounds, peers)), sem((rounds, peers)),
-            sem((rounds, peers)), sem((rounds, peers)),
-            sem((chan_local, peers, freq_count)), sem((chan_local, peers, freq_count)),
-            sem((max(steps, chan_local * freq_count),)),
+            pltpu.VMEM((chan_local, 2, half, 128), jnp.float32),
+            pltpu.VMEM((chan_local, half, 128), jnp.float32),
+            pltpu.VMEM((chan_local, half, 128), jnp.float32),
+            pltpu.VMEM((chan_local, line - 1, half, 128), jnp.float32),
+            pltpu.VMEM((2, half, 128), jnp.float32),
+            pltpu.VMEM((chan_local, 2 * k, 640), jnp.float32),
+            sem((tile_count,)), sem((tile_count,)), sem(()),
+            sem((tile_count, peers)), sem((tile_count, peers)),
+            sem((tile_count,)), sem((tile_count,)),
+            sem((chan_local,)), sem((chan_local,)),
+            sem((chan_local,)), sem((chan_local, line - 1)),
+            sem((chan_local,)), sem((chan_local,)),
+            sem((tile_count - 1,)), sem((chan_local,)),
+            sem((chan_local, line)), sem((chan_local, line)), sem((chan_local, line)),
+            sem((chan_local, line)), sem((chan_local, line)),
         ],
         compiler_params=pltpu.CompilerParams(
             collective_id=0, has_side_effects=True, vmem_limit_bytes=56 * 2**20
         ),
-    )(voltages, banded(coeffs), start)
-    return cleaned.astype(jnp.float32)
+    )(voltages, ids, start)
+    stride = tile_count * inputs_local
+    return pl.pallas_call(
+        finish_kernel,
+        grid=(freq_count,),
+        in_specs=[
+            pl.BlockSpec((tile_count, chan_local, rows, inputs_local), lambda f: (0, 0, 0, f)),
+            pl.BlockSpec((tile_count, chan_local, 2 * k, inputs_local), lambda f: (0, 0, 0, f)),
+            pl.BlockSpec((chan_local, 2 * k, rows), lambda f: (0, 0, 0)),
+        ],
+        out_specs=pl.BlockSpec((2, chan_local, spectra_local, stride), lambda f: (0, 0, 0, f)),
+        out_shape=jax.ShapeDtypeStruct((2, chan_local, spectra_local, freq_count * stride), jnp.float32),
+        compiler_params=pltpu.CompilerParams(vmem_limit_bytes=40 * 2**20),
+    )(own, q, left)
 
 
 def solution(mesh):

time: 102 us -> 70.2 us (0.69)
  Pallas kernels: 93.3 us -> 65.3 us
  other arithmetic: 5.49 us -> 0 us
  local copies, waits for them, and re-layouts: 2.22 us -> 4.62 us
    pallas_call x1, Pallas kernels: 93.3 us -> 62.3 us  [body(): pl.pallas_call(functools.partial(fused_kernel, k=k, freq=freq_count, tile...]
    convert_element_type x2 -> x0, other arithmetic: 2.95 us -> none  [the longest x1 2.93 us: body(): return cleaned.astype(jnp.float32)]
    pallas_call x0 -> x1, Pallas kernels: none -> 2.95 us  [body(): pl.pallas_call(finish_kernel, grid=(freq_count,), in_specs=[pl.BlockSpec(...]
    broadcast_in_dim x0 -> x3, local copies, waits for them, and re-layouts: none -> 1.48 us  [the longest x2 0.76 us: body(): jnp.broadcast_to(jnp.repeat(channel_ids, 2)[:, None], (2 * channels, P_SI...]
    unnamed x5 -> x6, local copies, waits for them, and re-layouts: 2.17 us -> 3.13 us
where the time goes in v1:
time: 70.2 us; the launch traced here: 69.9 us
  Pallas kernels  65.3 us (93%)
  local copies, waits for them, and re-layouts  4.62 us (7%)
    pallas_call x1, Pallas kernels, body(): pl.pallas_call(functools.partial(fused_kernel, k=k, freq=freq_count, tile...  62.3 us
    unnamed x6, local copies, waits for them, and re-layouts  3.13 us
    pallas_call x1, Pallas kernels, body(): pl.pallas_call(finish_kernel, grid=(freq_count,), in_specs=[pl.BlockSpec(...  2.95 us

profile of v1, /device:TPU:0, one launch (start us, length us, event | category | flops | bytes accessed | tf_op | source)
XLA Modules:
  0.0 69.9 jit_solution(13624104901754638599)
XLA Ops:
  0.0 0.7 %broadcast_in_dim.10 = s32[12,2]{1,0:T(8,128)S(1)} broadcast(s32[12]{0:T(128)} %param.4), dimensions={0} | broadcast | bytes 144 | tf_op jit(solution)/shard_map/broadcast_in_dim | solution.py:771
  0.7 0.1 broadcast_in_dim.11
  0.8 0.7 broadcast_in_dim.12.ids_ref
  1.5 62.3 %shard_map.37 = (bf16[8,3,48,512]{3,2,1,0:T(8,128)(2,1)}, f32[8,3,16,512]{3,2,1,0:T(8,128)}, f32[3,16,48]{2,1,0:T(8,128)}) custom-call(bf16[128,24960]{1,0:T(8,128)(2,1)} %volts_hbm.1, s32[24,128]{1,0:T(8,128)} %broadcast_in_dim.12.ids_ref, f32[16,4096]{1,0:T(8,128)} %bitcast.1), custom_call_target="tpu_custom_call" | custom-call | tf_op jit(solution)/shard_map/pallas_call | solution.py:778
  63.8 0.0 copy-start
  63.8 1.3 %copy-done = bf16[8,3,48,512]{3,2,1,0:T(8,128)(2,1)S(1)} copy-done((bf16[8,3,48,512]{3,2,1,0:T(8,128)(2,1)S(1)}, bf16[8,3,48,512]{3,2,1,0:T(8,128)(2,1)}, u32[]{:S(2)}) %copy-start) | copy-done | bytes 1179672
  65.1 0.0 copy-start.1
  65.1 1.1 %copy-done.1 = f32[8,3,16,512]{3,2,1,0:T(8,128)S(1)} copy-done((f32[8,3,16,512]{3,2,1,0:T(8,128)S(1)}, f32[8,3,16,512]{3,2,1,0:T(8,128)}, u32[]{:S(2)}) %copy-start.1) | copy-done | bytes 786456
  66.2 0.0 copy-start.2
  66.2 0.7 %copy-done.2 = f32[3,16,48]{2,1,0:T(8,128)S(1)} copy-done((f32[3,16,48]{2,1,0:T(8,128)S(1)}, f32[3,16,48]{2,1,0:T(8,128)}, u32[]{:S(2)}) %copy-start.2) | copy-done | bytes 9240
  67.0 2.9 %shard_map.38 = f32[2,3,24,4096]{3,2,1,0:T(8,128)} custom-call(bf16[8,3,48,512]{3,2,1,0:T(8,128)(2,1)S(1)} %copy-done, f32[8,3,16,512]{3,2,1,0:T(8,128)S(1)} %copy-done.1, f32[3,16,48]{2,1,0:T(8,128)S(1)} %copy-done.2), custom_call_target="tpu_custom_call" | custom-call | tf_op jit(solution)/shard_map/pallas_call | solution.py:814
Async XLA Ops:
  63.8 1.3 %copy-start = (bf16[8,3,48,512]{3,2,1,0:T(8,128)(2,1)S(1)}, bf16[8,3,48,512]{3,2,1,0:T(8,128)(2,1)}, u32[]{:S(2)}) copy-start(bf16[8,3,48,512]{3,2,1,0:T(8,128)(2,1)} %get-tuple-element.8.own_ref) | copy-start | bytes 3538948
  65.1 1.1 %copy-start.1 = (f32[8,3,16,512]{3,2,1,0:T(8,128)S(1)}, f32[8,3,16,512]{3,2,1,0:T(8,128)}, u32[]{:S(2)}) copy-start(f32[8,3,16,512]{3,2,1,0:T(8,128)} %get-tuple-element.9.q_ref) | copy-start | bytes 2359300
  66.2 0.7 %copy-start.2 = (f32[3,16,48]{2,1,0:T(8,128)S(1)}, f32[3,16,48]{2,1,0:T(8,128)}, u32[]{:S(2)}) copy-start(f32[3,16,48]{2,1,0:T(8,128)} %get-tuple-element.10.left_ref) | copy-start | bytes 27652

commit v2 on v1

--- a/solution.py
+++ b/solution.py
@@ -13,7 +13,7 @@
 ITERS = 3
 STEP = 16
 SUB = 8
-LAG = 4
+EARLY = 4
 
 loading = 0.5
 highest = lax.Precision.HIGHEST
@@ -154,7 +154,6 @@
         fetch(j).start()
 
     build_table(ids_ref, table_ref)
-    pl.semaphore_wait(barrier, freq - 1 + tile - 1)
 
     def rows_of(b):
         return pl.ds(pl.multiple_of(b * rows, rows), rows)
@@ -183,49 +182,59 @@
         pieces = [result[:, n * cols : (n + 1) * cols].reshape(-1, SUB, cols) for n in range(subs)]
         result = jnp.concatenate(pieces, axis=1)
         stage[j] = result.reshape(freq, chans, rows, cols).astype(jnp.bfloat16)
-        for d in range(1, freq):
-            handover(j, d).start()
-        own_part(j).start()
 
     def arrive(j):
         for d in range(1, freq):
             handover(j, d).wait_recv()
         own_part(j).wait()
 
-    def forward(b):
-        return remote(v_ref.at[:, rows_of(b), :], own_ref.at[me], z_send.at[b], z_recv.at[me], {"tile": b})
-
-    def keep(b):
-        return pltpu.make_async_copy(v_ref.at[:, rows_of(b), :], own_ref.at[me], mine_sem)
-
-    def pass_on(j):
+    def forward(j, d, b):
+        f = lax.rem(group + d, freq)
+        lanes = pl.ds(pl.multiple_of(f * cols, cols), cols)
+        src = stage.at[j, group] if d == 0 else v_ref.at[:, rows_of(block_at(j)), lanes]
+        return remote(src, own_ref.at[me, :, :, lanes], z_send.at[j, d], z_recv.at[me, f], {"tile": b})
+
+    def keep(j, d):
+        lanes = pl.ds(pl.multiple_of(lax.rem(group + d, freq) * cols, cols), cols)
+        src = stage.at[j, group] if d == 0 else v_ref.at[:, rows_of(block_at(j)), lanes]
+        return pltpu.make_async_copy(src, own_ref.at[me, :, :, lanes], mine_sem.at[d])
+
+    def pass_on(j, d):
         b = block_at(j)
 
         @pl.when(b != me)
         def _():
-            forward(b).start()
+            forward(j, d, b).start()
 
         @pl.when(b == me)
         def _():
-            keep(b).start()
-
-    def first(j, carry):
+            keep(j, d).start()
+
+    def compute(j, carry):
         filter_step(j)
         return carry
 
-    def both(j, carry):
-        filter_step(j)
-        arrive(j - LAG)
-        pass_on(j - LAG)
+    def dispatch(j, carry):
+        for d in range(1, freq):
+            handover(j, d).start()
+        own_part(j).start()
+        pass_on(j, 0)
         return carry
 
-    def last(j, carry):
+    def collect(j, carry):
         arrive(j)
+
+        @pl.when(j < EARLY)
+        def _():
+            for d in range(1, freq):
+                pass_on(j, d)
+
         return carry
 
-    lax.fori_loop(0, LAG, first, 0)
-    lax.fori_loop(LAG, tile, both, 0)
-    lax.fori_loop(tile - LAG, tile, last, 0)
+    lax.fori_loop(0, tile, compute, 0)
+    pl.semaphore_wait(barrier, freq - 1 + tile - 1)
+    lax.fori_loop(0, tile, dispatch, 0)
+    lax.fori_loop(0, tile, collect, 0)
 
     start = jnp.concatenate(
         [
@@ -287,8 +296,9 @@
             def _():
                 to_root(c, d).start()
 
-    for j in range(tile - LAG, tile):
-        pass_on(j)
+    for j in range(EARLY, tile):
+        for d in range(1, freq):
+            pass_on(j, d)
 
     g_re = exact(start_ref[...], start_ref[:k])
     g_im = exact(start_ref[...], start_ref[k:])
@@ -415,14 +425,20 @@
         for d in range(1, freq):
             handover(j, d).wait_send()
 
-        @pl.when(j != me)
+        b = block_at(j)
+
+        @pl.when(b != me)
         def _():
-            forward(j).wait_send()
-            remote(v_ref.at[:, rows_of(j), :], own_ref.at[j], z_send.at[j], z_recv.at[j], {"tile": j}).wait_recv()
-
-        @pl.when(j == me)
+            for d in range(freq):
+                forward(j, d, b).wait_send()
+                lanes = pl.ds(d * cols, cols)
+                piece = own_ref.at[b, :, :, lanes]
+                remote(piece, piece, z_send.at[j, d], z_recv.at[b, d], {"tile": b}).wait_recv()
+
+        @pl.when(b == me)
         def _():
-            keep(j).wait()
+            for d in range(freq):
+                keep(j, d).wait()
 
         return carry
 
@@ -451,7 +467,8 @@
 
 
 def build_table(ids_ref, table_ref):
-    count = ids_ref.shape[0]
+    channels = ids_ref.shape[0]
+    count = 2 * channels
     length = TAPS * P_SIZE
     tap = lax.broadcasted_iota(jnp.int32, (8, P_SIZE), 0)
     point = lax.broadcasted_iota(jnp.int32, (8, P_SIZE), 1)
@@ -464,7 +481,10 @@
     shape = shape / jnp.sqrt(total)
     part = lax.broadcasted_iota(jnp.int32, (count, P_SIZE), 0)
     place = lax.broadcasted_iota(jnp.int32, (count, P_SIZE), 1)
-    phases = jnp.bitwise_and(ids_ref[...] * place, P_SIZE - 1)
+    ids = jnp.zeros((count, P_SIZE), jnp.int32)
+    for c in range(channels):
+        ids = jnp.where(part // 2 == c, ids_ref[c], ids)
+    phases = jnp.bitwise_and(ids * place, P_SIZE - 1)
     angles = 2.0 * math.pi / P_SIZE * phases.astype(jnp.float32)
     rotors = jnp.where(jnp.bitwise_and(part, 1) == 0, jnp.cos(angles), -jnp.sin(angles))
     spread = []
@@ -768,7 +788,6 @@
     if spectra_all != 192 or spectra_local % SUB or tile_count % 4 or chan_local > 4 or k != 8:
         return body_split(voltages, channel_ids, start_basis)
 
-    ids = jnp.broadcast_to(jnp.repeat(channel_ids, 2)[:, None], (2 * channels, P_SIZE))
     start = start_basis.reshape(2 * k, freq_count * tile_count * inputs_local)
     rows = 2 * spectra_local
     line = tile_count // 2
@@ -777,7 +796,7 @@
     peers = freq_count - 1
     own, q, left = pl.pallas_call(
         functools.partial(fused_kernel, k=k, freq=freq_count, tile=tile_count),
-        in_specs=[pl.BlockSpec(memory_space=pl.ANY), VMEM, VMEM],
+        in_specs=[pl.BlockSpec(memory_space=pl.ANY), pl.BlockSpec(memory_space=pltpu.SMEM), VMEM],
         out_specs=[pl.BlockSpec(memory_space=pl.ANY), VMEM, VMEM],
         out_shape=[
             jax.ShapeDtypeStruct((tile_count, chan_local, rows, width), jnp.bfloat16),
@@ -796,9 +815,9 @@
             pltpu.VMEM((chan_local, line - 1, half, 128), jnp.float32),
             pltpu.VMEM((2, half, 128), jnp.float32),
             pltpu.VMEM((chan_local, 2 * k, 640), jnp.float32),
-            sem((tile_count,)), sem((tile_count,)), sem(()),
+            sem((tile_count,)), sem((tile_count,)), sem((freq_count,)),
             sem((tile_count, peers)), sem((tile_count, peers)),
-            sem((tile_count,)), sem((tile_count,)),
+            sem((tile_count, freq_count)), sem((tile_count, freq_count)),
             sem((chan_local,)), sem((chan_local,)),
             sem((chan_local,)), sem((chan_local, line - 1)),
             sem((chan_local,)), sem((chan_local,)),
@@ -809,7 +828,7 @@
         compiler_params=pltpu.CompilerParams(
             collective_id=0, has_side_effects=True, vmem_limit_bytes=56 * 2**20
         ),
-    )(voltages, ids, start)
+    )(voltages, channel_ids, start)
     stride = tile_count * inputs_local
     return pl.pallas_call(
         finish_kernel,
@@ -821,7 +840,7 @@
         ],
         out_specs=pl.BlockSpec((2, chan_local, spectra_local, stride), lambda f: (0, 0, 0, f)),
         out_shape=jax.ShapeDtypeStruct((2, chan_local, spectra_local, freq_count * stride), jnp.float32),
-        compiler_params=pltpu.CompilerParams(vmem_limit_bytes=40 * 2**20),
+        compiler_params=pltpu.CompilerParams(vmem_limit_bytes=60 * 2**20),
     )(own, q, left)
 
 

time: 70.2 us -> 69.3 us (0.987)
  local copies, waits for them, and re-layouts: 4.62 us -> 0 us
  Pallas kernels: 65.3 us -> 69.1 us
    unnamed x6 -> x0, local copies, waits for them, and re-layouts: 3.13 us -> none
    pallas_call x1, Pallas kernels: 62.3 us -> 64.6 us  [body(): pl.pallas_call(functools.partial(fused_kernel, k=k, freq=freq_count, tile...]
    pallas_call x1, Pallas kernels: 2.95 us -> 4.45 us  [body(): pl.pallas_call(finish_kernel, grid=(freq_count,), in_specs=[pl.BlockSpec(...]
    broadcast_in_dim x3 -> x0, local copies, waits for them, and re-layouts: 1.48 us -> none  [the longest x2 0.76 us: body(): jnp.broadcast_to(jnp.repeat(channel_ids, 2)[:, None], (2 * channels, P_SI...]
where the time goes in v2:
time: 69.3 us; the launch traced here: 69.1 us
  Pallas kernels  69.1 us (100%)
    pallas_call x1, Pallas kernels, body(): pl.pallas_call(functools.partial(fused_kernel, k=k, freq=freq_count, tile...  64.6 us
    pallas_call x1, Pallas kernels, body(): pl.pallas_call(finish_kernel, grid=(freq_count,), in_specs=[pl.BlockSpec(...  4.45 us

profile of v2, /device:TPU:0, one launch (start us, length us, event | category | flops | bytes accessed | tf_op | source)
XLA Modules:
  0.0 69.1 jit_solution(16690265563443070884)
XLA Ops:
  0.0 64.6 %shard_map.37 = (bf16[8,3,48,512]{3,2,1,0:T(8,128)(2,1)}, f32[8,3,16,512]{3,2,1,0:T(8,128)}, f32[3,16,48]{2,1,0:T(8,128)}) custom-call(bf16[128,24960]{1,0:T(8,128)(2,1)} %volts_hbm.1, s32[12]{0:T(128)} %ids_ref.1, f32[16,4096]{1,0:T(8,128)} %bitcast.1), custom_call_target="tpu_custom_call" | custom-call | tf_op jit(solution)/shard_map/pallas_call | solution.py:797
  64.6 4.4 %shard_map.38 = f32[2,3,24,4096]{3,2,1,0:T(8,128)} custom-call(bf16[8,3,48,512]{3,2,1,0:T(8,128)(2,1)} %get-tuple-element.8.own_ref, f32[8,3,16,512]{3,2,1,0:T(8,128)} %get-tuple-element.9.q_ref, f32[3,16,48]{2,1,0:T(8,128)} %get-tuple-element.10.left_ref), custom_call_target="tpu_custom_call" | custom-call | tf_op jit(solution)/shard_map/pallas_call | solution.py:833

commit v3 on v2

--- a/solution.py
+++ b/solution.py
@@ -14,6 +14,7 @@
 STEP = 16
 SUB = 8
 EARLY = 4
+AHEAD = 5
 
 loading = 0.5
 highest = lax.Precision.HIGHEST
@@ -118,7 +119,7 @@
     vol_ref, table_ref, stage, v_ref, parts_ref, pack_ref, pair_ref, half_ref, land_ref, full_ref, res_ref,
     vol_sem, own_sem, mine_sem, f_send, f_recv, z_send, z_recv,
     p_send, p_recv, k_send, k_recv, j_send, j_recv, b_send, b_recv,
-    up_send, down_send, line_recv, mate_send, mate_recv,
+    line_send, line_recv, mate_send, mate_recv,
     *, k, freq, tile,
 ):
     chans, _, spectra, width = parts_ref.shape
@@ -155,22 +156,15 @@
 
     build_table(ids_ref, table_ref)
 
-    def rows_of(b):
-        return pl.ds(pl.multiple_of(b * rows, rows), rows)
-
-    my_cols = pl.ds(pl.multiple_of(group * cols, cols), cols)
-
     def handover(j, d):
         peer = lax.rem(group + d, freq)
         return remote(
-            stage.at[j, peer], v_ref.at[:, rows_of(block_at(j)), my_cols],
+            stage.at[j, peer], v_ref.at[j, group],
             f_send.at[j, d - 1], f_recv.at[j, d - 1], {"freq": peer},
         )
 
     def own_part(j):
-        return pltpu.make_async_copy(
-            stage.at[j, group], v_ref.at[:, rows_of(block_at(j)), my_cols], own_sem.at[j]
-        )
+        return pltpu.make_async_copy(stage.at[j, group], v_ref.at[j, group], own_sem.at[j])
 
     def filter_step(j):
         fetch(j).wait()
@@ -190,14 +184,13 @@
 
     def forward(j, d, b):
         f = lax.rem(group + d, freq)
-        lanes = pl.ds(pl.multiple_of(f * cols, cols), cols)
-        src = stage.at[j, group] if d == 0 else v_ref.at[:, rows_of(block_at(j)), lanes]
-        return remote(src, own_ref.at[me, :, :, lanes], z_send.at[j, d], z_recv.at[me, f], {"tile": b})
+        src = stage.at[j, group] if d == 0 else v_ref.at[j, f]
+        return remote(src, own_ref.at[me, f], z_send.at[j, d], z_recv.at[me, f], {"tile": b})
 
     def keep(j, d):
-        lanes = pl.ds(pl.multiple_of(lax.rem(group + d, freq) * cols, cols), cols)
-        src = stage.at[j, group] if d == 0 else v_ref.at[:, rows_of(block_at(j)), lanes]
-        return pltpu.make_async_copy(src, own_ref.at[me, :, :, lanes], mine_sem.at[d])
+        f = lax.rem(group + d, freq)
+        src = stage.at[j, group] if d == 0 else v_ref.at[j, f]
+        return pltpu.make_async_copy(src, own_ref.at[me, f], mine_sem.at[d])
 
     def pass_on(j, d):
         b = block_at(j)
@@ -231,9 +224,14 @@
 
         return carry
 
-    lax.fori_loop(0, tile, compute, 0)
+    def pace(j, carry):
+        filter_step(j)
+        return dispatch(j, carry)
+
+    lax.fori_loop(0, AHEAD, compute, 0)
     pl.semaphore_wait(barrier, freq - 1 + tile - 1)
-    lax.fori_loop(0, tile, dispatch, 0)
+    lax.fori_loop(0, AHEAD, dispatch, 0)
+    lax.fori_loop(AHEAD, tile, pace, 0)
     lax.fori_loop(0, tile, collect, 0)
 
     start = jnp.concatenate(
@@ -260,9 +258,11 @@
         return remote(pack_ref.at[c, 1 - core], pair_ref.at[c], p_send.at[c], p_recv.at[c], {"tile": mate})
 
     for c in range(chans):
-        loose = v_ref[c].astype(jnp.float32).reshape(tile, 2, block, width)
-        real_v = loose[:, 0].reshape(spectra, width).astype(jnp.bfloat16)
-        imag_v = loose[:, 1].reshape(spectra, width).astype(jnp.bfloat16)
+        loose = [v_ref[:, f, c].astype(jnp.float32).reshape(tile, 2, block, cols) for f in range(freq)]
+        real_v, imag_v = [
+            jnp.concatenate([part[:, r].reshape(spectra, cols) for part in loose], axis=1).astype(jnp.bfloat16)
+            for r in range(2)
+        ]
         parts_ref[c, 0] = real_v
         parts_ref[c, 1] = imag_v
         k_re = nt(real_v, real_v) + nt(imag_v, imag_v)
@@ -346,32 +346,21 @@
         for d in range(1, tile):
             spread(at, d).start()
 
-    def line_copy(c, origin, to, sem):
-        slot = 2 * origin + core
+    def line_copy(c, d):
         return remote(
-            q_ref.at[slot, c], q_ref.at[slot, c], sem.at[c, origin], line_recv.at[c, origin], {"tile": 2 * to + core}
-        )
+            q_ref.at[me, c], q_ref.at[me, c], line_send.at[c, d - 1], line_recv.at[c, z],
+            {"tile": lax.rem(me + 2 * d, tile)},
+        )
+
+    def line_arrival(c, origin):
+        piece = q_ref.at[2 * origin + core, c]
+        return remote(piece, piece, line_send.at[c, 0], line_recv.at[c, origin], {"tile": 2 * origin + core})
 
     def mate_copy(c, origin):
         slot = 2 * origin + core
         return remote(
             q_ref.at[slot, c], q_ref.at[slot, c], mate_send.at[c, origin], mate_recv.at[c, origin], {"tile": mate}
         )
-
-    def send_on(c, origin, up, down):
-        if up:
-
-            @pl.when(z < line - 1)
-            def _():
-                line_copy(c, origin, z + 1, up_send).start()
-
-        if down:
-
-            @pl.when(z > 0)
-            def _():
-                line_copy(c, origin, z - 1, down_send).start()
-
-        mate_copy(c, origin).start()
 
     for c in range(chans):
 
@@ -387,39 +376,29 @@
         on_im = fold3(plain(parts, parts_ref[c, 1]))
         q = jnp.concatenate([on_re[:k] - on_im[k:], on_re[k:] + on_im[:k]], axis=0)
         q_ref[me, c] = q + mix(b[:k], b[k:], start, k)
-        send_on(c, z, True, True)
+        for d in (2, 1, 3) if line == 4 else range(1, line):
+            line_copy(c, d).start()
+        mate_copy(c, z).start()
         turned = jnp.concatenate([-w[k:], w[:k]], axis=0)
         chosen = jnp.zeros((2 * k, rows), jnp.float32)
-        for t in range(tile):
-            lanes = slice(t * block, (t + 1) * block)
+        for j in range(tile):
+            t = (j % 2) * (tile // 2) + j // 2
+            lanes = slice(j * block, (j + 1) * block)
             pair = jnp.concatenate([w[:, lanes], turned[:, lanes]], axis=1)
             chosen = jnp.where(me == t, pair, chosen)
         left_ref[c] = chosen
 
-    for d in range(1, line):
-        for c in range(chans):
-
-            @pl.when(z >= d)
-            def _():
-                line_copy(c, z - d, z, up_send).wait_recv()
-                send_on(c, z - d, True, False)
-
-            @pl.when(z + d < line)
-            def _():
-                line_copy(c, z + d, z, down_send).wait_recv()
-                send_on(c, z + d, False, True)
+    for c in range(chans):
+        for d in (1, 3, 2) if line == 4 else range(1, line):
+            origin = lax.rem(z + d, line)
+            line_arrival(c, origin).wait_recv()
+            mate_copy(c, origin).start()
 
     for c in range(chans):
         for origin in range(line):
             mate_copy(c, origin).wait()
-
-            @pl.when((z >= origin) & (z < line - 1))
-            def _():
-                line_copy(c, origin, z + 1, up_send).wait_send()
-
-            @pl.when((z <= origin) & (z > 0))
-            def _():
-                line_copy(c, origin, z - 1, down_send).wait_send()
+        for d in range(1, line):
+            line_copy(c, d).wait_send()
 
     def drain(j, carry):
         for d in range(1, freq):
@@ -431,8 +410,7 @@
         def _():
             for d in range(freq):
                 forward(j, d, b).wait_send()
-                lanes = pl.ds(d * cols, cols)
-                piece = own_ref.at[b, :, :, lanes]
+                piece = own_ref.at[b, d]
                 remote(piece, piece, z_send.at[j, d], z_recv.at[b, d], {"tile": b}).wait_recv()
 
         @pl.when(b == me)
@@ -559,7 +537,7 @@
 
 
 def finish_kernel(own_ref, q_ref, left_ref, out_ref):
-    tile, chans, rows, cols = own_ref.shape
+    tile, _, chans, rows, cols = own_ref.shape
     block = rows // 2
     n2 = q_ref.shape[2]
     for c in range(chans):
@@ -570,7 +548,7 @@
             s_right = jnp.concatenate(
                 [s3[:n2], s3[n2 : 2 * n2], s3[:n2], s3[n2 : 2 * n2], s3[2 * n2 :], s3[:n2]], axis=0
             )
-            cleaned = own_ref[t, c].astype(jnp.float32) - tn(w_left, s_right)
+            cleaned = own_ref[t, 0, c].astype(jnp.float32) - tn(w_left, s_right)
             out_ref[0, c, :, t * cols : (t + 1) * cols] = cleaned[:block]
             out_ref[1, c, :, t * cols : (t + 1) * cols] = cleaned[block:]
 
@@ -799,7 +777,7 @@
         in_specs=[pl.BlockSpec(memory_space=pl.ANY), pl.BlockSpec(memory_space=pltpu.SMEM), VMEM],
         out_specs=[pl.BlockSpec(memory_space=pl.ANY), VMEM, VMEM],
         out_shape=[
-            jax.ShapeDtypeStruct((tile_count, chan_local, rows, width), jnp.bfloat16),
+            jax.ShapeDtypeStruct((tile_count, freq_count, chan_local, rows, inputs_local), jnp.bfloat16),
             jax.ShapeDtypeStruct((tile_count, chan_local, 2 * k, width), jnp.float32),
             jax.ShapeDtypeStruct((chan_local, 2 * k, rows), jnp.float32),
         ],
@@ -807,7 +785,7 @@
             pltpu.VMEM((tile_count, inputs_local, (spectra_local + TAPS - 1) * P_SIZE), jnp.bfloat16),
             pltpu.VMEM((2 * channels * SUB, (SUB + TAPS - 1) * P_SIZE), jnp.bfloat16),
             pltpu.VMEM((tile_count, freq_count, chan_local, rows, inputs_local), jnp.bfloat16),
-            pltpu.VMEM((chan_local, tile_count * rows, width), jnp.bfloat16),
+            pltpu.VMEM((tile_count, freq_count, chan_local, rows, inputs_local), jnp.bfloat16),
             pltpu.VMEM((chan_local, 2, spectra_all, width), jnp.bfloat16),
             pltpu.VMEM((chan_local, 2, half, 128), jnp.float32),
             pltpu.VMEM((chan_local, half, 128), jnp.float32),
@@ -822,7 +800,7 @@
             sem((chan_local,)), sem((chan_local, line - 1)),
             sem((chan_local,)), sem((chan_local,)),
             sem((tile_count - 1,)), sem((chan_local,)),
-            sem((chan_local, line)), sem((chan_local, line)), sem((chan_local, line)),
+            sem((chan_local, line - 1)), sem((chan_local, line)),
             sem((chan_local, line)), sem((chan_local, line)),
         ],
         compiler_params=pltpu.CompilerParams(
@@ -834,7 +812,7 @@
         finish_kernel,
         grid=(freq_count,),
         in_specs=[
-            pl.BlockSpec((tile_count, chan_local, rows, inputs_local), lambda f: (0, 0, 0, f)),
+            pl.BlockSpec((tile_count, 1, chan_local, rows, inputs_local), lambda f: (0, f, 0, 0, 0)),
             pl.BlockSpec((tile_count, chan_local, 2 * k, inputs_local), lambda f: (0, 0, 0, f)),
             pl.BlockSpec((chan_local, 2 * k, rows), lambda f: (0, 0, 0)),
         ],

time: 69.3 us -> 66.2 us (0.955)
  Pallas kernels: 69.1 us -> 66 us
    pallas_call x1, Pallas kernels: 64.6 us -> 61.5 us  [body(): pl.pallas_call(functools.partial(fused_kernel, k=k, freq=freq_count, tile...]
where the time goes in v3:
time: 66.2 us; the launch traced here: 66 us
  Pallas kernels  66 us (100%)
    pallas_call x1, Pallas kernels, body(): pl.pallas_call(functools.partial(fused_kernel, k=k, freq=freq_count, tile...  61.5 us
    pallas_call x1, Pallas kernels, body(): pl.pallas_call(finish_kernel, grid=(freq_count,), in_specs=[pl.BlockSpec(...  4.43 us

profile of v3, /device:TPU:0, one launch (start us, length us, event | category | flops | bytes accessed | tf_op | source)
XLA Modules:
  0.0 66.0 jit_solution(8417313936969274166)
XLA Ops:
  0.0 61.5 %shard_map.37 = (bf16[8,4,3,48,128]{4,3,2,1,0:T(8,128)(2,1)}, f32[8,3,16,512]{3,2,1,0:T(8,128)}, f32[3,16,48]{2,1,0:T(8,128)}) custom-call(bf16[128,24960]{1,0:T(8,128)(2,1)} %volts_hbm.1, s32[12]{0:T(128)} %ids_ref.1, f32[16,4096]{1,0:T(8,128)} %bitcast.1), custom_call_target="tpu_custom_call" | custom-call | tf_op jit(solution)/shard_map/pallas_call | solution.py:775
  61.5 4.4 %shard_map.38 = f32[2,3,24,4096]{3,2,1,0:T(8,128)} custom-call(bf16[8,4,3,48,128]{4,3,2,1,0:T(8,128)(2,1)} %get-tuple-element.8.own_ref, f32[8,3,16,512]{3,2,1,0:T(8,128)} %get-tuple-element.9.q_ref, f32[3,16,48]{2,1,0:T(8,128)} %get-tuple-element.10.left_ref), custom_call_target="tpu_custom_call" | custom-call | tf_op jit(solution)/shard_map/pallas_call | solution.py:811

commit v4 on v3

--- a/solution.py
+++ b/solution.py
@@ -15,6 +15,7 @@
 SUB = 8
 EARLY = 4
 AHEAD = 5
+LATE = 6
 
 loading = 0.5
 highest = lax.Precision.HIGHEST
@@ -232,7 +233,6 @@
     pl.semaphore_wait(barrier, freq - 1 + tile - 1)
     lax.fori_loop(0, AHEAD, dispatch, 0)
     lax.fori_loop(AHEAD, tile, pace, 0)
-    lax.fori_loop(0, tile, collect, 0)
 
     start = jnp.concatenate(
         [
@@ -242,92 +242,119 @@
         axis=1,
     )
     start3 = split3(start)
-    fold = spectra - 128
-    half = pack_ref.shape[2]
-    keep_mask = lax.broadcasted_iota(jnp.int32, (spectra, spectra), 0) >= lax.broadcasted_iota(
-        jnp.int32, (spectra, spectra), 1
-    )
-    pad_lanes = 128 - fold
-
-    def folded(value):
-        count = value.shape[0] // 2
-        wide = jnp.concatenate([value[:, 128:], jnp.zeros((2 * count, pad_lanes), jnp.float32)], axis=1)
-        return wide[:count] + pltpu.roll(wide[count:], fold, 1)
-
-    def to_mate(c):
-        return remote(pack_ref.at[c, 1 - core], pair_ref.at[c], p_send.at[c], p_recv.at[c], {"tile": mate})
-
-    for c in range(chans):
-        loose = [v_ref[:, f, c].astype(jnp.float32).reshape(tile, 2, block, cols) for f in range(freq)]
-        real_v, imag_v = [
-            jnp.concatenate([part[:, r].reshape(spectra, cols) for part in loose], axis=1).astype(jnp.bfloat16)
-            for r in range(2)
-        ]
-        parts_ref[c, 0] = real_v
-        parts_ref[c, 1] = imag_v
-        k_re = nt(real_v, real_v) + nt(imag_v, imag_v)
-        k_im = nt(real_v, imag_v) - nt(imag_v, real_v)
-        packed = jnp.where(keep_mask, k_re, k_im)
-        on_re = fold3(nt(start3, real_v))
-        on_im = fold3(nt(start3, imag_v))
-        w = jnp.concatenate([on_re[:k] + on_im[k:], on_re[k:] - on_im[:k]], axis=0)
-        tail = 2 * half - (spectra + spectra // 2 + 3 * k)
-        everything = jnp.concatenate(
-            [packed[:, :128], folded(packed), w[:, :128], folded(w), jnp.zeros((tail, 128), jnp.float32)], axis=0
-        )
-        pack_ref[c] = everything.reshape(2, half, 128)
-        to_mate(c).start()
+    stages, heights, offsets, first = plan(spectra, block, k)
+
+    def at_stage(g):
+        return pl.ds(offsets[g], heights[g])
+
+    def to_mate(g, c):
+        return remote(
+            pack_ref.at[c, 1 - core, at_stage(g)], pair_ref.at[c, at_stage(g)],
+            p_send.at[g, c], p_recv.at[g, c], {"tile": mate},
+        )
 
     def root_line(c):
         return line // 2 - 1 + c % 2
 
-    def to_root(c, d):
+    def to_root(g, c, d):
         return remote(
-            half_ref.at[c], land_ref.at[c, d - 1], k_send.at[c], k_recv.at[c, d - 1],
-            {"tile": 2 * root_line(c) + core},
-        )
-
-    for c in range(chans):
-        to_mate(c).wait_recv()
-        half_ref[c] = pack_ref[c, core] + pair_ref[c]
-        for d in range(1, line):
-
-            @pl.when(z == (root_line(c) + d) % line)
-            def _():
-                to_root(c, d).start()
-
-    for j in range(EARLY, tile):
+            half_ref.at[c, at_stage(g)], land_ref.at[c, d - 1, at_stage(g)],
+            k_send.at[g, c], k_recv.at[g, c, d - 1], {"tile": 2 * root_line(c) + core},
+        )
+
+    def product(g, c):
+        low, high = stages[g]
+        n = (high - low) * block
+        loose = [
+            v_ref[:high, f, c].astype(jnp.float32).reshape(high, 2, block, cols) for f in range(freq)
+        ]
+        real_f, imag_f = [
+            jnp.concatenate([part[:, r].reshape(high * block, cols) for part in loose], axis=1) for r in range(2)
+        ]
+        if high == tile:
+            parts_ref[c, 0] = real_f.astype(jnp.bfloat16)
+            parts_ref[c, 1] = imag_f.astype(jnp.bfloat16)
+        real_n, imag_n = real_f[low * block :], imag_f[low * block :]
+        blank = jnp.zeros((128 - n, width), jnp.float32)
+        real_w = jnp.concatenate([real_n, blank], axis=0).astype(jnp.bfloat16)
+        imag_w = jnp.concatenate([imag_n, blank], axis=0).astype(jnp.bfloat16)
+        left_re, left_im = real_n.astype(jnp.bfloat16), imag_n.astype(jnp.bfloat16)
+        if low == 0:
+            k_re = nt(left_re, real_w) + nt(left_im, imag_w)
+            k_im = nt(left_re, imag_w) - nt(left_im, real_w)
+            row = lax.broadcasted_iota(jnp.int32, (n, 128), 0)
+            col = lax.broadcasted_iota(jnp.int32, (n, 128), 1)
+            body = [jnp.where(row >= col, k_re, k_im)]
+        else:
+            gap = [jnp.zeros((spectra - high * block, width), jnp.float32)] if high < tile else []
+            on_re = jnp.concatenate([real_f] + gap + [imag_f] + gap, axis=0).astype(jnp.bfloat16)
+            on_im = jnp.concatenate([imag_f] + gap + [-real_f] + gap, axis=0).astype(jnp.bfloat16)
+            wide = nt(left_re, on_re) + nt(left_im, on_im)
+            body = [wide[:, m : m + 128] for m in range(0, 2 * spectra, 128)]
+        on_re = fold3(nt(start3, real_w))
+        on_im = fold3(nt(start3, imag_w))
+        body += [on_re[:k] + on_im[k:], on_re[k:] - on_im[:k]]
+        tail = 2 * heights[g] - sum(piece.shape[0] for piece in body)
+        if tail:
+            body.append(jnp.zeros((tail, 128), jnp.float32))
+        pack_ref[c, :, at_stage(g)] = jnp.concatenate(body, axis=0).reshape(2, heights[g], 128)
+        to_mate(g, c).start()
+
+    for g, (low, high) in enumerate(stages):
+        lax.fori_loop(low, high, collect, 0)
+        for c in range(chans):
+            product(g, c)
+        for c in range(chans):
+            to_mate(g, c).wait_recv()
+            half_ref[c, at_stage(g)] = pack_ref[c, core, at_stage(g)] + pair_ref[c, at_stage(g)]
+            for d in range(1, line):
+
+                @pl.when(z == (root_line(c) + d) % line)
+                def _():
+                    to_root(g, c, d).start()
+
+    side = z - (line // 2 - 1)
+    at = side + 2 * core
+    is_root = (side >= 0) & (side < 2) & (at < chans)
+
+    def pass_rest(j, carry):
         for d in range(1, freq):
             pass_on(j, d)
+        return carry
+
+    lax.fori_loop(EARLY, LATE, pass_rest, 0)
+
+    @pl.when(jnp.logical_not(is_root))
+    def _():
+        lax.fori_loop(LATE, tile, pass_rest, 0)
 
     g_re = exact(start_ref[...], start_ref[:k])
     g_im = exact(start_ref[...], start_ref[k:])
     gram0 = jnp.concatenate([g_re[:k] + g_im[k:], g_im[:k] - g_re[k:]], axis=0)
 
-    def join(c):
-        return remote(half_ref.at[c], full_ref.at[core], j_send.at[c], j_recv.at[c], {"tile": mate})
-
-    for c in range(chans):
-
-        @pl.when(z == root_line(c))
-        def _():
-            total = half_ref[c]
-            for d in range(1, line):
-                to_root(c, d).wait_recv()
-                total = total + land_ref[c, d - 1]
-
-            @pl.when(core == c // 2)
+    def join(g, c):
+        return remote(
+            half_ref.at[c, at_stage(g)], full_ref.at[core, at_stage(g)], j_send.at[g, c], j_recv.at[g, c], {"tile": mate}
+        )
+
+    for g in range(len(stages)):
+        for c in range(chans):
+
+            @pl.when(z == root_line(c))
             def _():
-                full_ref[core] = total
-
-            @pl.when(core != c // 2)
-            def _():
-                half_ref[c] = total
-                join(c).start()
-
-    side = z - (line // 2 - 1)
-    at = side + 2 * core
-    is_root = (side >= 0) & (side < 2) & (at < chans)
+                total = half_ref[c, at_stage(g)]
+                for d in range(1, line):
+                    to_root(g, c, d).wait_recv()
+                    total = total + land_ref[c, d - 1, at_stage(g)]
+
+                @pl.when(core == c // 2)
+                def _():
+                    full_ref[core, at_stage(g)] = total
+
+                @pl.when(core != c // 2)
+                def _():
+                    half_ref[c, at_stage(g)] = total
+                    join(g, c).start()
 
     def spread(c, d):
         return remote(
@@ -340,11 +367,16 @@
 
             @pl.when(at == c)
             def _():
-                join(c).wait_recv()
-
-        res_ref[at] = iterate(full_ref[...].reshape(2 * half, 128), gram0, k, spectra)
+                for g in range(len(stages)):
+                    join(g, c).wait_recv()
+
+        pieces = [
+            full_ref[:, at_stage(g)].reshape(2 * heights[g], 128) for g in range(len(stages))
+        ]
+        res_ref[at] = iterate(pieces, stages, gram0, k, spectra, block)
         for d in range(1, tile):
             spread(at, d).start()
+        lax.fori_loop(LATE, tile, pass_rest, 0)
 
     def line_copy(c, d):
         return remote(
@@ -421,16 +453,17 @@
         return carry
 
     lax.fori_loop(0, tile, drain, 0)
-    for c in range(chans):
-        to_mate(c).wait_send()
-
-        @pl.when(z != root_line(c))
-        def _():
-            to_root(c, 1).wait_send()
-
-        @pl.when((z == root_line(c)) & (core != c // 2))
-        def _():
-            join(c).wait_send()
+    for g in range(len(stages)):
+        for c in range(chans):
+            to_mate(g, c).wait_send()
+
+            @pl.when(z != root_line(c))
+            def _():
+                to_root(g, c, 1).wait_send()
+
+            @pl.when((z == root_line(c)) & (core != c // 2))
+            def _():
+                join(g, c).wait_send()
 
     @pl.when(is_root)
     def _():
@@ -478,25 +511,42 @@
         table_ref[:, frame * P_SIZE : (frame + 1) * P_SIZE] = value.reshape(count * SUB, P_SIZE).astype(jnp.bfloat16)
 
 
-def iterate(full, gram0, k, spectra):
-    fold = spectra - 128
-    count = spectra // 2
-    lane = lax.broadcasted_iota(jnp.int32, (1, 128), 1)
-
-    def unfold(top, bent):
-        low = jnp.where(lane < fold, bent, 0.0)
-        high = jnp.where(lane < fold, pltpu.roll(bent, 128 - fold, 1), 0.0)
-        return jnp.concatenate([top, jnp.concatenate([low, high], axis=0)], axis=1)
-
-    packed = unfold(full[:spectra], full[spectra : spectra + count])
-    at = spectra + count
-    w = unfold(full[at : at + 2 * k], full[at + 2 * k : at + 3 * k])
-    packed = jnp.concatenate([packed, jnp.zeros((256 - spectra, 256), jnp.float32)], axis=0)
-    turned = packed.T
+def plan(spectra, block, k):
+    blocks = spectra // block
+    first = 128 // block
+    stages = [(0, first)] + [(j, j + 1) for j in range(first, blocks)]
+    heights = [up(first * block + 2 * k, 16) // 2]
+    heights += [up(2 * spectra // 128 * block + 2 * k, 16) // 2] * (blocks - first)
+    offsets = [sum(heights[:g]) for g in range(len(heights))]
+    return stages, heights, offsets, first * block
+
+
+def iterate(pieces, stages, gram0, k, spectra, block):
+    first = stages[0][1] * block
+    tiles = 2 * spectra // 128
+    wide = jnp.concatenate(
+        [
+            jnp.concatenate([piece[m * block : (m + 1) * block] for m in range(tiles)], axis=1)
+            for piece in pieces[1:]
+        ],
+        axis=0,
+    )
+    pad = 256 - spectra
+    side_pad = jnp.zeros((spectra - first, pad), jnp.float32)
+    foot = jnp.zeros((pad, 256), jnp.float32)
+    packed = jnp.concatenate([pieces[0][:first], jnp.zeros((first, 128), jnp.float32)], axis=1)
+    low_re = jnp.concatenate([packed, jnp.concatenate([wide[:, :spectra], side_pad], axis=1), foot], axis=0)
     row = lax.broadcasted_iota(jnp.int32, (256, 256), 0)
     col = lax.broadcasted_iota(jnp.int32, (256, 256), 1)
-    k_re = jnp.where(row >= col, packed, turned)
-    k_im = jnp.where(row < col, packed, jnp.where(row > col, -turned, 0.0))
+    turned = low_re.T
+    k_re = jnp.where(row >= col, low_re, turned)
+    low_im = jnp.concatenate(
+        [-turned[:first], jnp.concatenate([wide[:, spectra:], side_pad], axis=1), foot], axis=0
+    )
+    k_im = jnp.where(row > col, low_im, jnp.where(row < col, -low_im.T, 0.0))
+    w = [pieces[0][first : first + 2 * k, :first]]
+    w += [piece[tiles * block : tiles * block + 2 * k, :block] for piece in pieces[1:]]
+    w = jnp.concatenate(w + [jnp.zeros((2 * k, pad), jnp.float32)], axis=1)
     both = jnp.concatenate([k_re, k_im], axis=1)
     high = both.astype(jnp.bfloat16)
     rest = both - high.astype(jnp.float32)
@@ -522,12 +572,32 @@
         g_re = exact(w, u[:k])
         g_im = exact(w, u[k:])
         gram = jnp.concatenate([g_re[:k] + g_im[k:], g_im[:k] - g_re[k:]], axis=0) + loading * loading * held
-        m_re, m_im = inverse_factor(gram, k)
         grown = jnp.concatenate([y, w / spectra + loading * a, loading * b], axis=1)
-        grown = mix(m_re, m_im, grown, k)
+        grown = eliminate(gram, grown, k)
         w, a, b = grown[:, :256], grown[:, 256:512], grown[:, 512:]
         held = b_identity(n2, k)
     return jnp.concatenate([w, a, b], axis=1)
+
+
+def eliminate(gram, rows, k):
+    g_re, g_im = gram[:k], -gram[k:]
+    r_re, r_im = rows[:k], rows[k:]
+    row = lax.broadcasted_iota(jnp.int32, (k, 1), 0)
+    scale = jnp.zeros((k, 1), jnp.float32)
+    for j in range(k):
+        c_re, c_im = g_re[:, j : j + 1], g_im[:, j : j + 1]
+        pivot = c_re[j : j + 1]
+        scale = jnp.where(row == j, pivot, scale)
+        if j == k - 1:
+            break
+        l_re = jnp.where(row > j, c_re / pivot, 0.0)
+        l_im = jnp.where(row > j, c_im / pivot, 0.0)
+        a_re, a_im = g_re[j : j + 1], g_im[j : j + 1]
+        g_re, g_im = g_re - (l_re * a_re - l_im * a_im), g_im - (l_re * a_im + l_im * a_re)
+        b_re, b_im = r_re[j : j + 1], r_im[j : j + 1]
+        r_re, r_im = r_re - (l_re * b_re - l_im * b_im), r_im - (l_re * b_im + l_im * b_re)
+    scale = 1.0 / jnp.sqrt(scale)
+    return jnp.concatenate([r_re * scale, r_im * scale], axis=0)
 
 
 def b_identity(n2, k):
@@ -763,13 +833,14 @@
     spectra_local = spectra_all // tile_count
     k = start_basis.shape[1]
     width = freq_count * inputs_local
-    if spectra_all != 192 or spectra_local % SUB or tile_count % 4 or chan_local > 4 or k != 8:
+    if spectra_all != 192 or spectra_local % SUB or tile_count % 4 or tile_count <= 128 // spectra_local or chan_local > 4 or k != 8:
         return body_split(voltages, channel_ids, start_basis)
 
     start = start_basis.reshape(2 * k, freq_count * tile_count * inputs_local)
     rows = 2 * spectra_local
     line = tile_count // 2
-    half = up(spectra_all + spectra_all // 2 + 3 * k, 16) // 2
+    stages, heights, _, first = plan(spectra_all, spectra_local, k)
+    half, count = sum(heights), len(stages)
     sem = pltpu.SemaphoreType.DMA
     peers = freq_count - 1
     own, q, left = pl.pallas_call(
@@ -796,9 +867,9 @@
             sem((tile_count,)), sem((tile_count,)), sem((freq_count,)),
             sem((tile_count, peers)), sem((tile_count, peers)),
             sem((tile_count, freq_count)), sem((tile_count, freq_count)),
-            sem((chan_local,)), sem((chan_local,)),
-            sem((chan_local,)), sem((chan_local, line - 1)),
-            sem((chan_local,)), sem((chan_local,)),
+            sem((count, chan_local)), sem((count, chan_local)),
+            sem((count, chan_local)), sem((count, chan_local, line - 1)),
+            sem((count, chan_local)), sem((count, chan_local)),
             sem((tile_count - 1,)), sem((chan_local,)),
             sem((chan_local, line - 1)), sem((chan_local, line)),
             sem((chan_local, line)), sem((chan_local, line)),

time: 66.2 us -> 67.2 us (1.015)
  Pallas kernels: 66 us -> 67 us
    pallas_call x1, Pallas kernels: 61.5 us -> 62.6 us  [body(): pl.pallas_call(functools.partial(fused_kernel, k=k, freq=freq_count, tile...]
where the time goes in v4:
time: 67.2 us; the launch traced here: 67 us
  Pallas kernels  67 us (100%)
    pallas_call x1, Pallas kernels, body(): pl.pallas_call(functools.partial(fused_kernel, k=k, freq=freq_count, tile...  62.6 us
    pallas_call x1, Pallas kernels, body(): pl.pallas_call(finish_kernel, grid=(freq_count,), in_specs=[pl.BlockSpec(...  4.43 us

profile of v4, /device:TPU:0, one launch (start us, length us, event | category | flops | bytes accessed | tf_op | source)
XLA Modules:
  0.0 67.0 jit_solution(5752872775607524233)
XLA Ops:
  0.0 62.6 %shard_map.37 = (bf16[8,4,3,48,128]{4,3,2,1,0:T(8,128)(2,1)}, f32[8,3,16,512]{3,2,1,0:T(8,128)}, f32[3,16,48]{2,1,0:T(8,128)}) custom-call(bf16[128,24960]{1,0:T(8,128)(2,1)} %volts_hbm.1, s32[12]{0:T(128)} %ids_ref.1, f32[16,4096]{1,0:T(8,128)} %bitcast.1), custom_call_target="tpu_custom_call" | custom-call | tf_op jit(solution)/shard_map/pallas_call | solution.py:846
  62.6 4.4 %shard_map.38 = f32[2,3,24,4096]{3,2,1,0:T(8,128)} custom-call(bf16[8,4,3,48,128]{4,3,2,1,0:T(8,128)(2,1)} %get-tuple-element.8.own_ref, f32[8,3,16,512]{3,2,1,0:T(8,128)} %get-tuple-element.9.q_ref, f32[3,16,48]{2,1,0:T(8,128)} %get-tuple-element.10.left_ref), custom_call_target="tpu_custom_call" | custom-call | tf_op jit(solution)/shard_map/pallas_call | solution.py:882
